TPU v7x, 128 devices: a whole 4x4x4 slice. The times are simulated.
128 devices in a mesh: req: 32 (over y, x, core), tp: 4 (over z).
Axes of the slice: x: 4, y: 4, z: 4, core: 2. Of those that a mesh axis runs over, the one named last changes fastest.
Arguments:
- tokens: bfloat16 [256, 2048], P('req'), may hold values from -6 to 6
- first_gain: float32 [2048], replicated, may hold values from 0.1 to 1.9
- query_weight: bfloat16 [2048, 2048], P(None, 'tp'), may hold values from -0.125 to 0.125
- key_weight: bfloat16 [2048, 2048], P(None, 'tp'), may hold values from -0.125 to 0.125
- value_weight: bfloat16 [2048, 2048], P(None, 'tp'), may hold values from -0.125 to 0.125
- out_weight: bfloat16 [2048, 2048], P('tp'), may hold values from -0.125 to 0.125
- second_gain: float32 [2048], replicated, may hold values from 0.1 to 1.9
- up_weight: bfloat16 [2048, 8192], P(None, ('req', 'tp')), may hold values from -0.125 to 0.125
- down_weight: bfloat16 [8192, 2048], P(('req', 'tp')), may hold values from -0.0625 to 0.0625
- cache_keys: bfloat16 [131072, 2048], P('req', 'tp'), may hold values from -480 to 480
- cache_values: bfloat16 [131072, 2048], P('req', 'tp'), may hold values from -6 to 6
- lengths: int32 [256], replicated, may hold values from 1 to 8192, 131072 in all
- stream_order: int32 [256], replicated, may hold values from 0 to 255, each once
Outputs:
- hidden: bfloat16 [256, 2048], P('req', 'tp')
- new_keys: bfloat16 [256, 2048], P('req', 'tp')
- new_values: bfloat16 [256, 2048], P('req', 'tp')
Inputs may be any that keep to these rules, and one draw needn't show every extreme that they name: Every request's cache holds at least one row; the lengths sum to 131072 and the longest is exactly 8192. `stream_order`: each request appears exactly once.
All inputs are finite; a program needn't handle non-finite values.
Results may differ from a plain program's by a relative error of at most 0.0055.
The roundings to bfloat16 on the way count: a program that leaves them out, or rounds other values in their place, can miss the bound.
Values may be sent and summed in bfloat16 or wider, within the bound.
A program may use at most 128 MiB of HBM per device.

v0:
```python
import jax
import jax.numpy as jnp
from jax import lax
from jax.sharding import PartitionSpec as P

HEAD_DIM = 128


def merged_2(x, axis, combine):
    everything = jax.tree.map(lambda part: lax.all_gather(part, axis), x)
    first = jax.tree.map(lambda part: part[0], everything)

    def turn(k, so_far):
        return combine(so_far, jax.tree.map(lambda part: part[k], everything))

    return lax.fori_loop(1, lax.axis_size(axis), turn, first)


def layer_norm(values, gain_vector):
    center = jnp.mean(values, axis=-1, keepdims=True)
    shifted = values - center
    spread = jnp.mean(shifted * shifted, axis=-1, keepdims=True)
    return shifted * lax.rsqrt(spread + 1e-05) * gain_vector


def combine_parts(left_part, right_part):
    peak_left, mass_left, out_left = left_part
    peak_right, mass_right, out_right = right_part
    ceiling = jnp.maximum(peak_left, peak_right)
    scale_left = jnp.exp(peak_left - ceiling)
    scale_right = jnp.exp(peak_right - ceiling)
    mass_both = mass_left * scale_left + mass_right * scale_right
    out_both = out_left * jnp.repeat(scale_left, HEAD_DIM, axis=1) + out_right * jnp.repeat(
        scale_right, HEAD_DIM, axis=1
    )
    return (ceiling, mass_both, out_both)


def body(
    tokens,
    first_gain,
    query_weight,
    key_weight,
    value_weight,
    out_weight,
    second_gain,
    up_weight,
    down_weight,
    cache_keys,
    cache_values,
    lengths,
    stream_order,
):
    req_count = lax.axis_size("req")
    tp_count = lax.axis_size("tp")
    own_rows = tokens.shape[0]
    width = tokens.shape[1]
    head_width = query_weight.shape[1]
    local_heads = head_width // HEAD_DIM
    requests = own_rows * req_count
    cache_rows = cache_keys.shape[0]
    column_width = width // tp_count
    residual = tokens.astype(jnp.float32)
    normed = layer_norm(residual, first_gain).astype(jnp.bfloat16)
    queries = (
        jnp.dot(normed, query_weight, preferred_element_type=jnp.float32) * HEAD_DIM ** (-0.5)
    ).astype(jnp.bfloat16)
    new_keys = jnp.dot(normed, key_weight, preferred_element_type=jnp.float32).astype(jnp.bfloat16)
    new_values = jnp.dot(normed, value_weight, preferred_element_type=jnp.float32).astype(
        jnp.bfloat16
    )
    every_query = lax.all_gather(queries, "req", axis=0, tiled=True)
    stream_len = jnp.take(lengths, stream_order)
    bounds = jnp.cumsum(stream_len)
    positions = lax.axis_index("req") * cache_rows + jnp.arange(cache_rows, dtype=jnp.int32)
    slots = jnp.searchsorted(bounds, positions, side="right")
    row_owner = jnp.take(stream_order, slots)
    owner_ids = jnp.arange(requests, dtype=jnp.int32)
    member = row_owner[:, None] == owner_ids[None, :]
    select = member.astype(jnp.bfloat16)
    row_query = (
        jnp.dot(select, every_query, preferred_element_type=jnp.float32)
        .astype(jnp.bfloat16)
        .reshape(cache_rows, local_heads, HEAD_DIM)
    )
    key_rows = cache_keys.reshape(cache_rows, local_heads, HEAD_DIM)
    scores = jnp.einsum("rhd,rhd->rh", row_query, key_rows, preferred_element_type=jnp.float32)
    member_wide = member[:, :, None]
    peak = jnp.max(jnp.where(member_wide, scores[:, None, :], jnp.float32(-1e30)), axis=0)
    row_peak = jnp.sum(jnp.where(member_wide, peak[None, :, :], jnp.float32(0.0)), axis=1)
    expo = jnp.exp(scores - row_peak)
    mass = jnp.einsum(
        "pr,ph->rh", member.astype(jnp.float32), expo, precision=lax.Precision.HIGHEST
    )
    weights = expo.astype(jnp.bfloat16)
    masked_weights = jnp.transpose(select)[None, :, :] * jnp.transpose(weights)[:, None, :]
    value_rows = cache_values.reshape(cache_rows, local_heads, HEAD_DIM)
    partial_value = jnp.einsum(
        "hrp,phd->rhd", masked_weights, value_rows, preferred_element_type=jnp.float32
    ).reshape(requests, head_width)
    merged = merged_2((peak, mass, partial_value), "req", combine_parts)
    offset = lax.axis_index("req") * own_rows
    peak_own = lax.dynamic_slice_in_dim(merged[0], offset, own_rows, 0)
    mass_own = lax.dynamic_slice_in_dim(merged[1], offset, own_rows, 0)
    out_own = lax.dynamic_slice_in_dim(merged[2], offset, own_rows, 0)
    self_score = jnp.einsum(
        "rhd,rhd->rh",
        queries.reshape(own_rows, local_heads, HEAD_DIM),
        new_keys.reshape(own_rows, local_heads, HEAD_DIM),
        preferred_element_type=jnp.float32,
    )
    ceiling = jnp.maximum(peak_own, self_score)
    self_weight = jnp.exp(self_score - ceiling)
    older_weight = jnp.exp(peak_own - ceiling)
    total = self_weight + mass_own * older_weight
    summed = jnp.repeat(self_weight, HEAD_DIM, axis=1) * new_values.astype(
        jnp.float32
    ) + out_own * jnp.repeat(older_weight, HEAD_DIM, axis=1)
    attended = (summed / jnp.repeat(total, HEAD_DIM, axis=1)).astype(jnp.bfloat16)
    partial_middle = jnp.dot(attended, out_weight, preferred_element_type=jnp.float32)
    middle = residual + lax.psum(partial_middle, "tp")
    normed_two = layer_norm(middle, second_gain).astype(jnp.bfloat16)
    tp_offset = lax.axis_index("tp") * column_width
    unit_count = up_weight.shape[1]
    all_normed = lax.all_gather(normed_two, "req", axis=0, tiled=True)
    activation = jax.nn.gelu(
        jnp.dot(all_normed, up_weight, preferred_element_type=jnp.float32), approximate=False
    ).astype(jnp.bfloat16)
    shaped_act = activation.reshape(req_count, own_rows, unit_count)
    shaped_down = down_weight.reshape(unit_count, tp_count, column_width)
    term = jnp.einsum("arf,ftc->atrc", shaped_act, shaped_down, preferred_element_type=jnp.float32)
    term = term.reshape(req_count * tp_count, own_rows, column_width)
    mlp_out = lax.psum_scatter(term, ("req", "tp"), scatter_dimension=0, tiled=True).reshape(
        own_rows, column_width
    )
    middle_columns = lax.dynamic_slice_in_dim(middle, tp_offset, column_width, 1)
    hidden = (middle_columns + mlp_out).astype(jnp.bfloat16)
    return (hidden, new_keys, new_values)


def solution(mesh):
    return jax.shard_map(
        body,
        mesh=mesh,
        in_specs=(
            P("req", None),
            P(),
            P(None, "tp"),
            P(None, "tp"),
            P(None, "tp"),
            P("tp", None),
            P(),
            P(None, ("req", "tp")),
            P(("req", "tp"), None),
            P("req", "tp"),
            P("req", "tp"),
            P(),
            P(),
        ),
        out_specs=(P("req", "tp"), P("req", "tp"), P("req", "tp")),
        check_vma=False,
    )
```

profile of v0, /device:TPU:1, one launch (start us, length us, event | category | flops | bytes accessed | tf_op | source)
XLA Modules:
  0.0 1258.6 jit_solution(5008983148317732544)
XLA Ops:
  8.1 2.0 gather_fusion.1
  11.4 232.6 %while.44 = (s32[]{:T(128)}, u32[4096]{0:T(1024)S(1)}, u32[4096]{0:T(1024)S(1)}, s32[256]{0:T(256)S(1)}, s32[]{:T(128)}, /*index=5*/s32[]{:T(128)}, s32[]{:T(128)}, s32[]{}) while((s32[]{:T(128)}, u32[4096]{0:T(1024)S(1)}, u32[4096]{0:T(1024)S(1)}, s32[256]{0:T(256)S(1)}, s32[]{:T(128)}, /*index=5*/s32[]{:T(128)}, s32[]{:T(128)}, ...), condition=%wide.region_5.6_spmd.clone, body=%wide.region_4.5_spmd.clone.sunk | while | flops 81924 | bytes 254073 | solution.py:76
  11.4 25.7 %gather_fusion = s32[4096]{0:T(1024)S(1)} fusion(s32[256]{0:T(256)S(1)} %get-tuple-element.441, u32[4096]{0:T(1024)S(1)} %broadcast_clamp_fusion.2), kind=kCustom, calls=%fused_computation.clone.clone.1 | custom fusion | bytes 49152 | tf_op jit(solution)/shard_map/jit(searchsorted)/jit(_searchsorted_scan_impl)/vmap(jit(_searchsorted_scan_impl))/while/body/eval_jaxpr/gather | solution.py:76
  37.2 25.7 %gather_fusion = s32[4096]{0:T(1024)S(1)} fusion(s32[256]{0:T(256)S(1)} %get-tuple-element.441, u32[4096]{0:T(1024)S(1)} %broadcast_clamp_fusion.2), kind=kCustom, calls=%fused_computation.clone.clone.1 | custom fusion | bytes 49152 | tf_op jit(solution)/shard_map/jit(searchsorted)/jit(_searchsorted_scan_impl)/vmap(jit(_searchsorted_scan_impl))/while/body/eval_jaxpr/gather | solution.py:76
  63.1 25.7 %gather_fusion = s32[4096]{0:T(1024)S(1)} fusion(s32[256]{0:T(256)S(1)} %get-tuple-element.441, u32[4096]{0:T(1024)S(1)} %broadcast_clamp_fusion.2), kind=kCustom, calls=%fused_computation.clone.clone.1 | custom fusion | bytes 49152 | tf_op jit(solution)/shard_map/jit(searchsorted)/jit(_searchsorted_scan_impl)/vmap(jit(_searchsorted_scan_impl))/while/body/eval_jaxpr/gather | solution.py:76
  88.9 25.7 %gather_fusion = s32[4096]{0:T(1024)S(1)} fusion(s32[256]{0:T(256)S(1)} %get-tuple-element.441, u32[4096]{0:T(1024)S(1)} %broadcast_clamp_fusion.2), kind=kCustom, calls=%fused_computation.clone.clone.1 | custom fusion | bytes 49152 | tf_op jit(solution)/shard_map/jit(searchsorted)/jit(_searchsorted_scan_impl)/vmap(jit(_searchsorted_scan_impl))/while/body/eval_jaxpr/gather | solution.py:76
  114.7 25.7 %gather_fusion = s32[4096]{0:T(1024)S(1)} fusion(s32[256]{0:T(256)S(1)} %get-tuple-element.441, u32[4096]{0:T(1024)S(1)} %broadcast_clamp_fusion.2), kind=kCustom, calls=%fused_computation.clone.clone.1 | custom fusion | bytes 49152 | tf_op jit(solution)/shard_map/jit(searchsorted)/jit(_searchsorted_scan_impl)/vmap(jit(_searchsorted_scan_impl))/while/body/eval_jaxpr/gather | solution.py:76
  140.6 25.7 %gather_fusion = s32[4096]{0:T(1024)S(1)} fusion(s32[256]{0:T(256)S(1)} %get-tuple-element.441, u32[4096]{0:T(1024)S(1)} %broadcast_clamp_fusion.2), kind=kCustom, calls=%fused_computation.clone.clone.1 | custom fusion | bytes 49152 | tf_op jit(solution)/shard_map/jit(searchsorted)/jit(_searchsorted_scan_impl)/vmap(jit(_searchsorted_scan_impl))/while/body/eval_jaxpr/gather | solution.py:76
  166.4 25.7 %gather_fusion = s32[4096]{0:T(1024)S(1)} fusion(s32[256]{0:T(256)S(1)} %get-tuple-element.441, u32[4096]{0:T(1024)S(1)} %broadcast_clamp_fusion.2), kind=kCustom, calls=%fused_computation.clone.clone.1 | custom fusion | bytes 49152 | tf_op jit(solution)/shard_map/jit(searchsorted)/jit(_searchsorted_scan_impl)/vmap(jit(_searchsorted_scan_impl))/while/body/eval_jaxpr/gather | solution.py:76
  192.3 25.7 %gather_fusion = s32[4096]{0:T(1024)S(1)} fusion(s32[256]{0:T(256)S(1)} %get-tuple-element.441, u32[4096]{0:T(1024)S(1)} %broadcast_clamp_fusion.2), kind=kCustom, calls=%fused_computation.clone.clone.1 | custom fusion | bytes 49152 | tf_op jit(solution)/shard_map/jit(searchsorted)/jit(_searchsorted_scan_impl)/vmap(jit(_searchsorted_scan_impl))/while/body/eval_jaxpr/gather | solution.py:76
  218.1 25.7 %gather_fusion = s32[4096]{0:T(1024)S(1)} fusion(s32[256]{0:T(256)S(1)} %get-tuple-element.441, u32[4096]{0:T(1024)S(1)} %broadcast_clamp_fusion.2), kind=kCustom, calls=%fused_computation.clone.clone.1 | custom fusion | bytes 49152 | tf_op jit(solution)/shard_map/jit(searchsorted)/jit(_searchsorted_scan_impl)/vmap(jit(_searchsorted_scan_impl))/while/body/eval_jaxpr/gather | solution.py:76
  244.6 25.7 %gather_fusion.2 = s32[4096]{0:T(1024)S(1)} fusion(s32[256]{0:T(256)S(1)} %copy-done.1, s32[4096]{0:T(1024)S(1)} %fusion.36), kind=kCustom, calls=%fused_computation.2 | custom fusion | bytes 49152 | tf_op jit(solution)/shard_map/jit(_take)/gather | solution.py:77
  270.4 1.9 iota_compare_fusion.1
  272.3 1.8 fusion.9
  274.4 2.0 fusion.13
  276.4 26.7 %all_gather.21 = bf16[256,512]{1,0:T(8,128)(2,1)S(1)} all-gather(bf16[8,512]{1,0:T(8,128)(2,1)S(1)} %fusion.13), channel_id=1, replica_groups=mesh['req'=32,'tp'=4] {'req'}, dimensions={0}, use_global_device_ids=true | all-gather | bytes 270336 | tf_op jit(solution)/shard_map/all_gather | solution.py:72
  303.1 3.1 convolution_convert_fusion
  306.2 7.9 copy.58
  314.1 6.9 reshape.166
  321.1 10.3 multiply_reduce_fusion
  331.4 2.2 copy.59
  333.6 3.0 select_reduce_fusion.1
  336.7 2.6 select_reduce_fusion
  339.2 6.4 copy.62
  345.7 5.7 fusion.5
  352.4 24.5 %all-gather = f32[8192,4]{0,1:T(4,128)S(1)} all-gather(f32[256,4]{0,1:T(4,128)S(1)} %select_reduce_fusion.1), channel_id=2, replica_groups=mesh['req'=32,'tp'=4] {'req'}, dimensions={0}, use_global_device_ids=true | all-gather | bytes 135168 | tf_op jit(solution)/shard_map/all_gather | solution.py:10
  376.9 1.4 fusion.10
  378.3 25.0 %all-gather.1 = f32[8192,4]{0,1:T(4,128)} all-gather(f32[256,4]{0,1:T(4,128)S(1)} %fusion.10), channel_id=3, replica_groups=mesh['req'=32,'tp'=4] {'req'}, dimensions={0}, use_global_device_ids=true | all-gather | bytes 135168 | tf_op jit(solution)/shard_map/all_gather | solution.py:10
  404.0 2.1 convolution_convert_fusion.1
  406.1 2.8 fusion.35
  408.9 16.3 %all-gather.5.cloned.1.call-done = f32[32,256,512]{2,1,0:T(8,128)} async-done(((f32[1,256,512]{2,1,0:T(8,128)}), f32[32,256,512]{2,1,0:T(8,128)}) %all-gather.5.cloned.1.call-update) | async-done | bytes 16777232 | tf_op jit(solution)/shard_map/all_gather | solution.py:10
  426.4 95.0 %while.43 = (s32[]{:T(128)}, f32[256,4]{0,1:T(4,128)S(1)}, f32[256,4]{0,1:T(4,128)S(1)}, f32[256,512]{1,0:T(8,128)S(1)}, f32[32,256,4]{1,2,0:T(4,128)S(1)}, /*in...) while((s32[]{:T(128)}, f32[256,4]{0,1:T(4,128)S(1)}, ...), condition=%wide.region_9.10_spmd, body=%wide.region_8.9_spmd.sunk | while | flops 399365 | bytes 3727511 | solution.py:16
  428.0 1.4 fusion.64
  440.3 1.4 fusion.64
  443.4 1.4 fusion.64
  449.5 1.4 fusion.64
  455.6 1.4 fusion.64
  461.8 1.4 fusion.64
  495.5 1.4 fusion.64
  501.6 1.4 fusion.64
  510.8 1.4 fusion.64
  513.9 1.4 fusion.64
  520.0 1.4 fusion.64
  522.6 38.7 %all-reduce.2.cloned.1.call-done = f32[8,2048]{1,0:T(8,128)} async-done(((f32[8,2048]{1,0:T(8,128)}), f32[8,2048]{1,0:T(8,128)}) %all-reduce.2.cloned.1.call-update) | async-done | bytes 65552 | tf_op jit(solution)/shard_map/psum | solution.py:121
  563.3 45.4 %all-gather.7.cloned.1.call-done = bf16[256,2048]{1,0:T(8,128)(2,1)} async-done(((bf16[8,2048]{1,0:T(8,128)(2,1)}), bf16[256,2048]{1,0:T(8,128)(2,1)}) %all-gather.7.cloned.1.call-update) | async-done | bytes 1048592 | tf_op jit(solution)/shard_map/all_gather | solution.py:125
  608.7 1.8 fusion.23
  610.6 1.8 fusion.14
  612.4 638.3 %reduce-scatter.2.cloned.1.call-done = f32[1,8,512]{2,1,0:T(8,128)} async-done(((f32[128,8,512]{2,1,0:T(8,128)}), f32[1,8,512]{2,1,0:T(8,128)}) %reduce-scatter.2.cloned.1.call-update) | async-done | bytes 16400 | tf_op jit(solution)/shard_map/reduce_scatter | solution.py:133
  (263 shorter events, 89.6 us)
Async XLA Ops:
  7.2 514.3 %copy-start = (bf16[512,2048]{1,0:T(8,128)(2,1)S(1)}, bf16[512,2048]{1,0:T(8,128)(2,1)}, u32[]{:S(2)}) copy-start(bf16[512,2048]{1,0:T(8,128)(2,1)} %param.22) | copy-start | bytes 6291460
  7.2 418.1 %all-gather.5.cloned.1.call-start = ((), (), s32[]{:S(2)}) async-start(), calls=%async_computation.1 | async-start | bytes 17301504 | tf_op jit(solution)/shard_map/all_gather | solution.py:10
  243.9 0.7 copy-start.1
  244.6 29.5 %copy-start.2 = (bf16[8,2048]{1,0:T(8,128)(2,1)S(1)}, bf16[8,2048]{1,0:T(8,128)(2,1)}, u32[]{:S(2)}) copy-start(bf16[8,2048]{1,0:T(8,128)(2,1)} %param.17) | copy-start | bytes 98308
  244.6 29.8 %copy-start.4 = (f32[2048]{0:T(1024)S(1)}, f32[2048]{0:T(1024)}, u32[]{:S(2)}) copy-start(f32[2048]{0:T(1024)} %param.18) | copy-start | bytes 24580
  352.4 208.9 %all-reduce.2.cloned.1.call-start = ((), (), s32[]{:S(2)}) async-start(), calls=%async_computation.2 | async-start | bytes 131072 | tf_op jit(solution)/shard_map/psum | solution.py:121
  406.1 115.4 %copy-start.5 = (bf16[8,512]{1,0:T(8,128)(2,1)}, bf16[8,512]{1,0:T(8,128)(2,1)S(1)}, u32[]{:S(2)}) copy-start(bf16[8,512]{1,0:T(8,128)(2,1)S(1)} %convolution_convert_fusion.1) | copy-start | bytes 24580
  426.3 136.2 %copy-start.6 = (f32[2048]{0:T(1024)S(1)}, f32[2048]{0:T(1024)}, u32[]{:S(2)}) copy-start(f32[2048]{0:T(1024)} %param.23) | copy-start | bytes 24580
  521.4 89.2 %copy-start.3 = (bf16[64,2048]{1,0:T(8,128)(2,1)S(1)}, bf16[64,2048]{1,0:T(8,128)(2,1)}, u32[]{:S(2)}) copy-start(bf16[64,2048]{1,0:T(8,128)(2,1)} %param.25) | copy-start | bytes 786436
  522.6 86.1 %all-gather.7.cloned.1.call-start = ((), (), s32[]{:S(2)}) async-start(), calls=%async_computation.3 | async-start | bytes 1081344 | tf_op jit(solution)/shard_map/all_gather | solution.py:125
  563.2 687.5 %reduce-scatter.2.cloned.1.call-start = ((), (), s32[]{:S(2)}) async-start(), calls=%async_computation.4 | async-start | bytes 2113536 | tf_op jit(solution)/shard_map/reduce_scatter | solution.py:133
Sparse Core Ops, SparseCore 0:
  352.5 72.7 all-gather.4
  522.7 38.5 all-reduce.1
  563.6 45.0 all-gather.6
  612.5 638.1 reduce-scatter.1
where the time goes:
time: 1270 us; the launch traced here: 1260 us
  waiting for transfers between devices  739 us (58%)
  local copies, waits for them, and re-layouts  316 us (25%)
  other arithmetic  90.2 us (7%)
  blocking collectives  76.2 us (6%)
  matrix products  21.8 us (2%)
  between operations  13.9 us (1%)
    reduce_scatter x1, waiting for transfers between devices, body(): lax.psum_scatter(term, ('req', 'tp'), scatter_dimension=0, tiled=True)  638 us
    gather x9, local copies, waits for them, and re-layouts, body(): slots = jnp.searchsorted(bounds, positions, side='right')  232 us
    all_gather x2, blocking collectives, merged_2(): everything = jax.tree.map(lambda part: lax.all_gather(part, axis), x)  49.5 us
    all_gather x1, waiting for transfers between devices, body(): all_normed = lax.all_gather(normed_two, 'req', axis=0, tiled=True)  45.4 us
    add x31, other arithmetic, combine_parts(): out_left * jnp.repeat(scale_left, HEAD_DIM, axis=1)  42.8 us
    psum x1, waiting for transfers between devices, body(): middle = residual + lax.psum(partial_middle, 'tp')  38.7 us
    all_gather x1, blocking collectives, body(): every_query = lax.all_gather(queries, 'req', axis=0, tiled=True)  26.7 us
    gather x1, local copies, waits for them, and re-layouts, body(): row_owner = jnp.take(stream_order, slots)  25.7 us
  transfers between devices with their start and end apart: 4, of which 4 were waited for; matrix products, arithmetic and copies ran while one was open for 1% of the time, Pallas kernels for 0%

commit v1 on v0

v1 whole, which is shorter than its diff:
```python
import functools

import jax
import jax.numpy as jnp
from jax import lax
from jax.experimental import pallas as pl
from jax.experimental.pallas import tpu as pltpu
from jax.sharding import PartitionSpec as P

HEAD = 128
MESH = pl.DeviceIdType.MESH
NEG = -1e30
WIN = 32
CHUNK = 512
NT = (((1,), (1,)), ((), ()))


def norm(v, g):
    center = jnp.mean(v, axis=-1, keepdims=True)
    shifted = v - center
    spread = jnp.mean(shifted * shifted, axis=-1, keepdims=True)
    return shifted * lax.rsqrt(spread + 1e-05) * g


def dot(a, b):
    return jnp.dot(a, b, preferred_element_type=jnp.float32)


def each(lo, hi, f):
    def step(i, carry):
        f(i)
        return carry

    lax.fori_loop(lo, hi, step, 0)


def project(n, tok, gain, lens, order, wq, wk, wv, q_all, nk, nv, tab, wb, qs, wsem, ss, rs):
    me, z = lax.axis_index("req"), lax.axis_index("tp")
    part = wq.shape[0] // 4
    loads = [
        pltpu.make_async_copy(
            wq.at[pl.ds(i * part, part)], wb.at[0, pl.ds(i * part, part)], wsem.at[i]
        )
        for i in range(4)
    ]
    loads += [
        pltpu.make_async_copy(wk, wb.at[1], wsem.at[4]),
        pltpu.make_async_copy(wv, wb.at[2], wsem.at[5]),
    ]
    for load in loads:
        load.start()
    barrier = pltpu.get_barrier_semaphore()

    def greet(d):
        peer = lax.rem(me + d, n)
        pl.semaphore_signal(barrier, inc=1, device_id=(peer, z), device_id_type=MESH)

    each(1, n, greet)
    normed = norm(tok[...].astype(jnp.float32), gain[...]).astype(jnp.bfloat16)
    q = jnp.zeros((tok.shape[0], wq.shape[1]), jnp.float32)
    for i in range(4):
        loads[i].wait()
        q += dot(normed[:, i * part : (i + 1) * part], wb[0, i * part : (i + 1) * part])
    q = (q * HEAD**-0.5).astype(jnp.bfloat16)
    qs[...] = q
    q_all[me] = q
    pl.semaphore_wait(barrier, n - 1)

    def send(d):
        peer = lax.rem(me + d, n)
        pltpu.make_async_remote_copy(
            qs, q_all.at[me], ss.at[d], rs.at[me], device_id=(peer, z), device_id_type=MESH
        ).start()

    each(1, n, send)
    loads[4].wait()
    nk[...] = dot(normed, wb[1]).astype(jnp.bfloat16)
    loads[5].wait()
    nv[...] = dot(normed, wb[2]).astype(jnp.bfloat16)
    m = lens.shape[1]
    sub = lax.broadcasted_iota(jnp.int32, (m, m), 0).astype(jnp.float32)
    lane = lax.broadcasted_iota(jnp.int32, (m, m), 1).astype(jnp.float32)
    len_l = lens[...].astype(jnp.float32)
    ord_s = jnp.sum(
        jnp.where(sub == lane, order[...].astype(jnp.float32), 0.0), axis=1, keepdims=True
    )
    hot = ord_s == lane
    rank = jnp.sum(jnp.where(hot, sub, 0.0), axis=0, keepdims=True)
    len_s = jnp.sum(jnp.where(hot, len_l, 0.0), axis=1, keepdims=True)
    end = jnp.sum(jnp.where(sub <= rank, len_s, 0.0), axis=0, keepdims=True)
    tab[0:1] = rank
    tab[1:2] = end - len_l
    tab[2:3] = end
    tab[3:8] = jnp.zeros((5, m), jnp.float32)

    def finish(d):
        src = lax.rem(me + d, n)
        copy = pltpu.make_async_remote_copy(
            qs, q_all.at[src], ss.at[d], rs.at[src], device_id=(src, z), device_id_type=MESH
        )
        copy.wait_recv()
        copy.wait_send()

    each(1, n, finish)


def attend(q_all, tab, nk_in, nv_in, keys, values, part, nk, nv, kb, vb, sc, acc, ksem, vsem):
    rows, width = keys.shape
    heads = width // HEAD
    steps = rows // CHUNK
    span = lambda i: pl.ds(i * CHUNK, CHUNK)
    kl = [pltpu.make_async_copy(keys.at[span(i)], kb.at[span(i)], ksem.at[i]) for i in range(steps)]
    vl = [
        pltpu.make_async_copy(values.at[span(i)], vb.at[span(i)], vsem.at[i]) for i in range(steps)
    ]
    for load in kl + vl:
        load.start()
    nk[...] = nk_in[...]
    nv[...] = nv_in[...]
    base = lax.axis_index("req") * rows
    base_f = base.astype(jnp.float32)
    rank, first, end = tab[0:1], tab[1:2], tab[2:3]
    m = rank.shape[1]
    sub = lax.broadcasted_iota(jnp.int32, (m, m), 0)
    lane = lax.broadcasted_iota(jnp.int32, (m, m), 1)
    diag = sub == lane
    upright = lambda row: jnp.sum(jnp.where(diag, row, 0.0), axis=1, keepdims=True)
    rank_s = upright(rank)
    here = jnp.logical_and(first < base_f + rows, end > base_f)
    here_s = upright(jnp.where(here, 1.0, 0.0)) > 0.5
    low = jnp.min(jnp.where(here, rank, 1e9)).astype(jnp.int32)
    high = jnp.max(jnp.where(here, rank, -1.0)).astype(jnp.int32)
    every_q = q_all[...].astype(jnp.float32).reshape(m, width).astype(jnp.bfloat16)
    tall = WIN * heads
    block = (
        lax.broadcasted_iota(jnp.int32, (tall, width), 0) // WIN
        == lax.broadcasted_iota(jnp.int32, (tall, width), 1) // HEAD
    )
    spot = lax.broadcasted_iota(jnp.int32, (WIN, HEAD), 1)

    def window(slot, opening):
        slot_f = slot.astype(jnp.float32)
        pick = rank == slot_f + lax.broadcasted_iota(jnp.int32, (WIN, m), 0).astype(jnp.float32)
        pick_f = jnp.where(pick, 1.0, 0.0)
        q = dot(pick_f.astype(jnp.bfloat16), every_q)
        first_w = jnp.sum(pick_f * first, axis=1, keepdims=True) - base_f
        end_w = jnp.sum(pick_f * end, axis=1, keepdims=True) - base_f
        first_t = jnp.concatenate([first_w] * heads, axis=0)
        end_t = jnp.concatenate([end_w] * heads, axis=0)
        q_block = jnp.where(block, jnp.concatenate([q] * heads, axis=0), 0.0).astype(jnp.bfloat16)
        top = jnp.full((tall, HEAD), NEG, jnp.float32)
        for i in range(steps):
            if opening:
                kl[i].wait()
            s = lax.dot_general(
                q_block, kb[i * CHUNK : (i + 1) * CHUNK], NT, preferred_element_type=jnp.float32
            )
            at = lax.broadcasted_iota(jnp.int32, (tall, CHUNK), 1).astype(jnp.float32) + float(
                i * CHUNK
            )
            s = jnp.where(jnp.logical_and(at >= first_t, at < end_t), s, NEG)
            sc[:, i * CHUNK : (i + 1) * CHUNK] = s
            for j in range(CHUNK // HEAD):
                top = jnp.maximum(top, s[:, j * HEAD : (j + 1) * HEAD])
        peak = jnp.max(top, axis=1, keepdims=True)
        held = jnp.zeros((tall, HEAD), jnp.float32)
        for i in range(steps):
            if opening:
                vl[i].wait()
            s = sc[:, i * CHUNK : (i + 1) * CHUNK]
            e = jnp.where(s > 0.1 * NEG, jnp.exp(s - peak), 0.0)
            for j in range(CHUNK // HEAD):
                held += e[:, j * HEAD : (j + 1) * HEAD]
            o = dot(e.astype(jnp.bfloat16), vb[i * CHUNK : (i + 1) * CHUNK])
            if i == 0:
                acc[...] = o
            else:
                acc[...] += o
        mass = jnp.sum(held, axis=1, keepdims=True)
        cut = lambda a, h: a[h * WIN : (h + 1) * WIN]
        stat = jnp.zeros((WIN, HEAD), jnp.float32)
        for h in range(heads):
            stat = jnp.where(spot == h, cut(peak, h), stat)
            stat = jnp.where(spot == heads + h, cut(mass, h), stat)
        found = jnp.concatenate(
            [
                acc[h * WIN : (h + 1) * WIN, h * HEAD : (h + 1) * HEAD] for h in range(heads)
            ]
            + [stat],
            axis=1,
        )
        put = rank_s == slot_f + lax.broadcasted_iota(jnp.int32, (m, WIN), 1).astype(jnp.float32)
        put = jnp.where(put, 1.0, 0.0).astype(jnp.bfloat16)
        one = found.astype(jnp.bfloat16)
        rest = found - one.astype(jnp.float32)
        two = rest.astype(jnp.bfloat16)
        three = (rest - two.astype(jnp.float32)).astype(jnp.bfloat16)
        placed = (dot(put, one) + dot(put, two)) + dot(put, three)
        if opening:
            part[...] = placed
        else:
            part[...] += placed

    window(low, True)
    each(1, (high - low) // WIN + 1, lambda w: window(low + w * WIN, False))
    stat = part[:, width:]
    lanes = lax.broadcasted_iota(jnp.int32, stat.shape, 1)
    part[:, width:] = jnp.where(
        jnp.logical_and(lanes < heads, jnp.logical_not(here_s)), NEG, stat
    )


def tail(
    n, t, nx, part, q_all, nk, nv, tok, gain, wo, up, down, hid,
    got, wob, upb, dnb, zs, zr, mc, ns, nr, ts, rr,
    lsem, a_s, a_r, u_s, u_r, d_s, d_r, z_s, z_r, n_s, n_r, r_s, r_r,
):
    me, z = lax.axis_index("req"), lax.axis_index("tp")
    ny = n // (2 * nx)
    y, x, c = me // (2 * nx), lax.rem(me // 2, nx), lax.rem(me, 2)
    nj = 2 * ny
    j0 = y * 2 + c
    k0 = j0 * t + z
    nk0 = nj * t
    width = q_all.shape[2]
    heads = width // HEAD
    own = tok.shape[0]

    def home(j):
        return ((j // 2) * nx + x) * 2 + lax.rem(j, 2)

    loads = [
        pltpu.make_async_copy(wo, wob, lsem.at[0]),
        pltpu.make_async_copy(up, upb.at[x], lsem.at[1]),
        pltpu.make_async_copy(down, dnb.at[x], lsem.at[2]),
        pltpu.make_async_copy(part.at[me], got.at[me], lsem.at[3]),
    ]
    for load in loads:
        load.start()
    barrier = pltpu.get_barrier_semaphore()

    def greet(d):
        peer = lax.rem(me + d, n)
        pl.semaphore_signal(barrier, inc=1, device_id=(peer, z), device_id_type=MESH)

    each(1, n, greet)

    def greet_plane(i):
        pz = lax.rem(z + 1 + i // nj, t)
        pl.semaphore_signal(
            barrier, inc=1, device_id=(home(lax.rem(i, nj)), pz), device_id_type=MESH
        )

    each(0, nj * (t - 1), greet_plane)
    pl.semaphore_wait(barrier, n - 1 + nj * (t - 1))

    def partial_copy(d, src, peer):
        return pltpu.make_async_remote_copy(
            part.at[peer], got.at[src], a_s.at[d], a_r.at[src],
            device_id=(peer, z), device_id_type=MESH,
        )

    each(1, n, lambda d: partial_copy(d, me, lax.rem(me + d, n)).start())

    def weight_copies(d, src):
        peer = (y * nx + lax.rem(x + d, nx)) * 2 + c
        return [
            pltpu.make_async_remote_copy(
                up, upb.at[src], u_s.at[d], u_r.at[src], device_id=(peer, z), device_id_type=MESH
            ),
            pltpu.make_async_remote_copy(
                down, dnb.at[src], d_s.at[d], d_r.at[src], device_id=(peer, z), device_id_type=MESH
            ),
        ]

    def weights_out(d):
        for copy in weight_copies(d, x):
            copy.start()

    each(1, nx, weights_out)

    q = q_all[me].astype(jnp.float32)
    kn = nk[...].astype(jnp.float32)
    vn = nv[...].astype(jnp.float32)
    spot = lax.broadcasted_iota(jnp.int32, (own, HEAD), 1)
    mine = jnp.zeros((own, HEAD), jnp.float32)
    for h in range(heads):
        cols = slice(h * HEAD, (h + 1) * HEAD)
        mine = jnp.where(spot == h, jnp.sum(q[:, cols] * kn[:, cols], axis=1, keepdims=True), mine)
    loads[3].wait()

    def partial_in(d):
        copy = partial_copy(d, lax.rem(me + d, n), lax.rem(me + d, n))
        copy.wait_recv()
        copy.wait_send()

    each(1, n, partial_in)
    stat = got[:, :, width:]
    top = jnp.maximum(jnp.max(stat, axis=0), mine)
    scale = jnp.exp(stat - top[None])
    mass = pltpu.roll(stat, HEAD - heads, axis=2)
    self_w = jnp.exp(mine - top)
    total = self_w + jnp.sum(scale * mass, axis=0)
    pieces = []
    for h in range(heads):
        cols = slice(h * HEAD, (h + 1) * HEAD)
        older = jnp.sum(got[:, :, cols] * scale[:, :, h : h + 1], axis=0)
        pieces.append((self_w[:, h : h + 1] * vn[:, cols] + older) / total[:, h : h + 1])
    attended = jnp.concatenate(pieces, axis=1).astype(jnp.bfloat16)
    loads[0].wait()
    pm = dot(attended, wob[...])
    zs[...] = pm
    zr[z] = pm

    def middle_copy(d, src):
        return pltpu.make_async_remote_copy(
            zs, zr.at[src], z_s.at[d], z_r.at[src],
            device_id=(me, lax.rem(z + d, t)), device_id_type=MESH,
        )

    each(1, t, lambda d: middle_copy(d, z).start())

    def middle_in(d):
        copy = middle_copy(d, lax.rem(z + d, t))
        copy.wait_recv()
        copy.wait_send()

    each(1, t, middle_in)
    mid = zr[0]
    for i in range(1, t):
        mid += zr[i]
    mid += tok[...].astype(jnp.float32)
    for i in range(t):
        mc[i] = mid[:, i * width : (i + 1) * width]
    normed = norm(mid, gain[...]).astype(jnp.bfloat16)
    ns[...] = normed
    nr[j0] = normed

    def normed_copy(d, src):
        return pltpu.make_async_remote_copy(
            ns, nr.at[src], n_s.at[d], n_r.at[src],
            device_id=(home(lax.rem(j0 + d, nj)), z), device_id_type=MESH,
        )

    each(1, nj, lambda d: normed_copy(d, j0).start())

    def normed_in(d):
        copy = normed_copy(d, lax.rem(j0 + d, nj))
        copy.wait_recv()
        copy.wait_send()

    each(1, nj, normed_in)
    loads[1].wait()
    loads[2].wait()

    def weights_in(d):
        for copy in weight_copies(d, lax.rem(x + d, nx)):
            copy.wait_recv()
            copy.wait_send()

    each(1, nx, weights_in)
    tokens, units, wide = nj * own, nx * up.shape[0], up.shape[1]
    rows = nr[...].astype(jnp.float32).reshape(tokens, wide).astype(jnp.bfloat16)
    pre = lax.dot_general(
        rows, upb[...].reshape(units, wide), NT, preferred_element_type=jnp.float32
    )
    act = (0.5 * pre * (1.0 + lax.erf(pre * 0.5**0.5))).astype(jnp.bfloat16)
    for i in range(t):
        cols = slice(i * width, (i + 1) * width)
        term = dot(act, dnb[:, :, cols].reshape(units, width))
        ts[:, i] = term.reshape(nj, own, width)
    rr[k0] = ts[j0, z]

    def term_copy(d, src):
        k = lax.rem(k0 + d, nk0)
        return pltpu.make_async_remote_copy(
            ts.at[k // t, lax.rem(k, t)], rr.at[src], r_s.at[d], r_r.at[src],
            device_id=(home(k // t), lax.rem(k, t)), device_id_type=MESH,
        )

    each(1, nk0, lambda d: term_copy(d, k0).start())

    def term_in(d):
        copy = term_copy(d, lax.rem(k0 + d, nk0))
        copy.wait_recv()
        copy.wait_send()

    each(1, nk0, term_in)
    hid[...] = (mc[z] + jnp.sum(rr[...], axis=0)).astype(jnp.bfloat16)


def body(
    n, t, nx, tokens, first_gain, query_weight, key_weight, value_weight, out_weight, second_gain,
    up_weight, down_weight, cache_keys, cache_values, lengths, stream_order,
):
    f32, b16 = jnp.float32, jnp.bfloat16
    own, wide = tokens.shape
    width = query_weight.shape[1]
    requests = own * n
    units = up_weight.shape[1]
    rows = cache_keys.shape[0]
    steps = rows // CHUNK
    vmem = pl.BlockSpec(memory_space=pltpu.VMEM)
    hbm = pl.BlockSpec(memory_space=pl.ANY)
    dma = pltpu.SemaphoreType.DMA
    shape = jax.ShapeDtypeStruct
    q_all, nk, nv, tab = pl.pallas_call(
        functools.partial(project, n),
        out_shape=(
            shape((n, own, width), b16),
            shape((own, width), b16),
            shape((own, width), b16),
            shape((8, requests), f32),
        ),
        in_specs=[vmem] * 4 + [hbm] * 3,
        out_specs=(vmem,) * 4,
        scratch_shapes=[
            pltpu.VMEM((3, wide, width), b16),
            pltpu.VMEM((own, width), b16),
            dma((6,)),
            dma((n,)),
            dma((n,)),
        ],
        compiler_params=pltpu.CompilerParams(collective_id=0, has_side_effects=True),
        name="project",
    )(
        tokens, first_gain.reshape(1, wide), lengths.reshape(1, requests),
        stream_order.reshape(1, requests), query_weight, key_weight, value_weight,
    )
    part, new_keys, new_values = pl.pallas_call(
        attend,
        out_shape=(
            shape((requests, width + HEAD), f32),
            shape((own, width), b16),
            shape((own, width), b16),
        ),
        in_specs=[vmem] * 4 + [hbm] * 2,
        out_specs=(vmem,) * 3,
        scratch_shapes=[
            pltpu.VMEM((rows, width), b16),
            pltpu.VMEM((rows, width), b16),
            pltpu.VMEM((WIN * width // HEAD, rows), f32),
            pltpu.VMEM((WIN * width // HEAD, width), f32),
            dma((steps,)),
            dma((steps,)),
        ],
        name="attend",
    )(q_all, tab, nk, nv, cache_keys, cache_values)
    nj = n // nx
    hidden = pl.pallas_call(
        functools.partial(tail, n, t, nx),
        out_shape=shape((own, width), b16),
        in_specs=[hbm] + [vmem] * 5 + [hbm] * 3,
        out_specs=vmem,
        scratch_shapes=[
            pltpu.VMEM((n, own, width + HEAD), f32),
            pltpu.VMEM((width, wide), b16),
            pltpu.VMEM((nx, units, wide), b16),
            pltpu.VMEM((nx, units, wide), b16),
            pltpu.VMEM((own, wide), f32),
            pltpu.VMEM((t, own, wide), f32),
            pltpu.VMEM((t, own, width), f32),
            pltpu.VMEM((own, wide), b16),
            pltpu.VMEM((nj, own, wide), b16),
            pltpu.VMEM((nj, t, own, width), f32),
            pltpu.VMEM((nj * t, own, width), f32),
            dma((4,)),
            dma((n,)), dma((n,)),
            dma((nx,)), dma((nx,)),
            dma((nx,)), dma((nx,)),
            dma((t,)), dma((t,)),
            dma((nj,)), dma((nj,)),
            dma((nj * t,)), dma((nj * t,)),
        ],
        compiler_params=pltpu.CompilerParams(collective_id=1, has_side_effects=True),
        name="tail",
    )(
        part.reshape(n, own, width + HEAD), q_all, new_keys, new_values, tokens,
        second_gain.reshape(1, wide), out_weight, up_weight.T, down_weight,
    )
    return hidden, new_keys, new_values


def solution(mesh):
    n, t = mesh.shape["req"], mesh.shape["tp"]
    return jax.shard_map(
        functools.partial(body, n, t, 4),
        mesh=mesh,
        in_specs=(
            P("req", None), P(), P(None, "tp"), P(None, "tp"), P(None, "tp"), P("tp", None), P(),
            P(None, ("req", "tp")), P(("req", "tp"), None), P("req", "tp"), P("req", "tp"), P(), P(),
        ),
        out_specs=(P("req", "tp"), P("req", "tp"), P("req", "tp")),
        check_vma=False,
    )
```

time: 1270 us -> 75.7 us (0.06)
  waiting for transfers between devices: 739 us -> 0 us
  local copies, waits for them, and re-layouts: 316 us -> 1.3 us
  other arithmetic: 90.2 us -> 0 us
  blocking collectives: 76.2 us -> 0 us
  Pallas kernels: 0 us -> 73.5 us
  matrix products: 21.8 us -> 0 us
  between operations: 13.9 us -> 0.66 us
    reduce_scatter x1 -> x0, waiting for transfers between devices: 638 us -> none  [body(): lax.psum_scatter(term, ('req', 'tp'), scatter_dimension=0, tiled=True)]
    gather x11 -> x0, local copies, waits for them, and re-layouts: 259 us -> none  [the longest x9 232 us: body(): slots = jnp.searchsorted(bounds, positions, side='right')]
    all_gather x3 -> x0, blocking collectives: 76.2 us -> none  [the longest x2 49.5 us: merged_2(): everything = jax.tree.map(lambda part: lax.all_gather(part, axis), x)]
    pallas_call x0 -> x3, Pallas kernels: none -> 73.5 us  [the longest x1 51.9 us: body(): pl.pallas_call(functools.partial(tail, n, t, nx), out_shape=shape((own, w...]
    add x63 -> x0, other arithmetic: 64.7 us -> none  [the longest x31 42.8 us: combine_parts(): out_left * jnp.repeat(scale_left, HEAD_DIM, axis=1)]
    all_gather x2 -> x0, waiting for transfers between devices: 61.7 us -> none  [the longest x1 45.4 us: body(): all_normed = lax.all_gather(normed_two, 'req', axis=0, tiled=True)]
    psum x1 -> x0, waiting for transfers between devices: 38.7 us -> none  [body(): middle = residual + lax.psum(partial_middle, 'tp')]
    dot_general x9 -> x0, matrix products: 21.8 us -> none  [the longest x1 5.68 us: body(): jnp.einsum('hrp,phd->rhd', masked_weights, value_rows, preferred_element_...]
  transfers between devices with their start and end apart: 4 -> 0, of which waited for: 4 -> 0; matrix products, arithmetic and copies ran while one was open for 1% -> 0% of each run, Pallas kernels for 0% -> 0%
where the time goes in v1:
time: 75.7 us; the launch traced here: 75.5 us
  Pallas kernels  73.5 us (97%)
  local copies, waits for them, and re-layouts  1.3 us (2%)
    pallas_call x1, Pallas kernels, body(): pl.pallas_call(functools.partial(tail, n, t, nx), out_shape=shape((own, w...  51.9 us
    pallas_call x1, Pallas kernels, body(): pl.pallas_call(functools.partial(project, n), out_shape=(shape((n, own, w...  14.3 us
    pallas_call x1, Pallas kernels, body(): pl.pallas_call(attend, out_shape=(shape((requests, width + HEAD), f32), s...  7.27 us

profile of v1, /device:TPU:1, one launch (start us, length us, event | category | flops | bytes accessed | tf_op | source)
XLA Modules:
  0.0 75.5 jit_solution(14127666347994913942)
XLA Ops:
  0.6 14.3 %project.1 = (bf16[32,8,512]{2,1,0:T(8,128)(2,1)}, bf16[8,512]{1,0:T(8,128)(2,1)}, bf16[8,512]{1,0:T(8,128)(2,1)}, f32[8,256]{1,0:T(8,128)}) custom-call(bf16[8,2048]{1,0:T(8,128)(2,1)} %tok.3, f32[1,2048]{1,0:T(1,128)} %bitcast.8, s32[1,256]{1,0:T(1,128)} %bitcast.10, s32[1,256]{1,0:T(1,128)} %bitcast.11, bf16[2048,512]{1,0:T(8,128)(2,1)} %wq.1, ...), custom_call_target="tpu_custom_call" | custom-call | tf_op jit(solution)/shard_map/project/pallas_call | solution.py:407
  15.0 7.3 %attend.1 = (f32[256,640]{1,0:T(8,128)}, bf16[8,512]{1,0:T(8,128)(2,1)}, bf16[8,512]{1,0:T(8,128)(2,1)}) custom-call(bf16[32,8,512]{2,1,0:T(8,128)(2,1)} %get-tuple-element.10.q_all, f32[8,256]{1,0:T(8,128)} %get-tuple-element.11.tab, bf16[8,512]{1,0:T(8,128)(2,1)} %get-tuple-element.12.nk_in, bf16[8,512]{1,0:T(8,128)(2,1)} %get-tuple-element.13.nv_in, ...), custom_call_target="tpu_custom_call" | custom-call | tf_op jit(solution)/shard_map/attend/pallas_call | solution.py:430
  22.2 51.9 %tail.1 = bf16[8,512]{1,0:T(8,128)(2,1)} custom-call(f32[32,8,640]{2,1,0:T(8,128)} %bitcast.6, bf16[32,8,512]{2,1,0:T(8,128)(2,1)} %get-tuple-element.10.q_all, bf16[8,512]{1,0:T(8,128)(2,1)} %get-tuple-element.21.nk, bf16[8,512]{1,0:T(8,128)(2,1)} %get-tuple-element.22.nv, bf16[8,2048]{1,0:T(8,128)(2,1)} %tok.3, f32[1,2048]{1,0:T(1,128)} %bitcast.9, ...), custom_call_target="tpu_custom_call" | custom-call | tf_op jit(solution)/shard_map/tail/pallas_call | solution.py:450
  74.2 1.3 %copy.17 = bf16[8,512]{1,0:T(8,128)(2,1)} copy(bf16[8,512]{1,0:T(8,128)(2,1)} %tail.1) | data formatting | bytes 16384

commit v2 on v1

--- a/solution.py
+++ b/solution.py
@@ -12,6 +12,7 @@
 NEG = -1e30
 WIN = 32
 CHUNK = 512
+VMEM_PROJECT, VMEM_ATTEND, VMEM_TAIL = 20 << 20, 16 << 20, 16 << 20
 NT = (((1,), (1,)), ((), ()))
 
 
@@ -34,9 +35,17 @@
     lax.fori_loop(lo, hi, step, 0)
 
 
-def project(n, tok, gain, lens, order, wq, wk, wv, q_all, nk, nv, tab, wb, qs, wsem, ss, rs):
+def project(
+    n, nx, tok_h, gain_h, lens_h, order_h, wq, wk, wv, keys, values, up,
+    q_all, nk, nv, tab, kb, vb, un,
+    tok, gain, lens, order, wb, qs, wsem, ss, rs, us, ur,
+):
     me, z = lax.axis_index("req"), lax.axis_index("tp")
     part = wq.shape[0] // 4
+    small = [
+        pltpu.make_async_copy(a, b, wsem.at[8 + i])
+        for i, (a, b) in enumerate([(tok_h, tok), (gain_h, gain), (lens_h, lens), (order_h, order)])
+    ]
     loads = [
         pltpu.make_async_copy(
             wq.at[pl.ds(i * part, part)], wb.at[0, pl.ds(i * part, part)], wsem.at[i]
@@ -46,8 +55,10 @@
     loads += [
         pltpu.make_async_copy(wk, wb.at[1], wsem.at[4]),
         pltpu.make_async_copy(wv, wb.at[2], wsem.at[5]),
+        pltpu.make_async_copy(keys, kb, wsem.at[6]),
+        pltpu.make_async_copy(values, vb, wsem.at[7]),
     ]
-    for load in loads:
+    for load in small + loads[:4]:
         load.start()
     barrier = pltpu.get_barrier_semaphore()
 
@@ -56,11 +67,15 @@
         pl.semaphore_signal(barrier, inc=1, device_id=(peer, z), device_id_type=MESH)
 
     each(1, n, greet)
+    small[0].wait()
+    small[1].wait()
     normed = norm(tok[...].astype(jnp.float32), gain[...]).astype(jnp.bfloat16)
     q = jnp.zeros((tok.shape[0], wq.shape[1]), jnp.float32)
     for i in range(4):
         loads[i].wait()
         q += dot(normed[:, i * part : (i + 1) * part], wb[0, i * part : (i + 1) * part])
+    for load in loads[4:]:
+        load.start()
     q = (q * HEAD**-0.5).astype(jnp.bfloat16)
     qs[...] = q
     q_all[me] = q
@@ -73,10 +88,15 @@
         ).start()
 
     each(1, n, send)
+    sides = side_copies(up, un, us, ur, me, z, nx)
+    for copy in sides:
+        copy.start()
     loads[4].wait()
     nk[...] = dot(normed, wb[1]).astype(jnp.bfloat16)
     loads[5].wait()
     nv[...] = dot(normed, wb[2]).astype(jnp.bfloat16)
+    small[2].wait()
+    small[3].wait()
     m = lens.shape[1]
     sub = lax.broadcasted_iota(jnp.int32, (m, m), 0).astype(jnp.float32)
     lane = lax.broadcasted_iota(jnp.int32, (m, m), 1).astype(jnp.float32)
@@ -102,19 +122,42 @@
         copy.wait_send()
 
     each(1, n, finish)
-
-
-def attend(q_all, tab, nk_in, nv_in, keys, values, part, nk, nv, kb, vb, sc, acc, ksem, vsem):
-    rows, width = keys.shape
+    loads[6].wait()
+    loads[7].wait()
+    for copy in sides:
+        copy.wait()
+
+
+def along(me, d, nx):
+    x = lax.rem(me // 2, nx)
+    return me + (lax.rem(x + d, nx) - x) * 2
+
+
+def side_copies(src, dst, ss, rs, me, z, nx):
+    return [
+        pltpu.make_async_remote_copy(
+            src, dst.at[i], ss.at[i], rs.at[i],
+            device_id=(along(me, d, nx), z), device_id_type=MESH,
+        )
+        for i, d in enumerate((1, nx - 1))
+    ]
+
+
+def relay_copies(slots, dst, ss, rs, me, z, nx):
+    half = dst.shape[0] // 2
+    return [
+        pltpu.make_async_remote_copy(
+            slots.at[i, pl.ds(i * half, half)], dst.at[pl.ds(i * half, half)], ss.at[i], rs.at[i],
+            device_id=(along(me, d, nx), z), device_id_type=MESH,
+        )
+        for i, d in enumerate((1, nx - 1))
+    ]
+
+
+def attend(q_all, tab, nk_in, nv_in, kb, vb, part, nk, nv, sc, acc, put_all):
+    rows, width = kb.shape
     heads = width // HEAD
     steps = rows // CHUNK
-    span = lambda i: pl.ds(i * CHUNK, CHUNK)
-    kl = [pltpu.make_async_copy(keys.at[span(i)], kb.at[span(i)], ksem.at[i]) for i in range(steps)]
-    vl = [
-        pltpu.make_async_copy(values.at[span(i)], vb.at[span(i)], vsem.at[i]) for i in range(steps)
-    ]
-    for load in kl + vl:
-        load.start()
     nk[...] = nk_in[...]
     nv[...] = nv_in[...]
     base = lax.axis_index("req") * rows
@@ -150,8 +193,6 @@
         q_block = jnp.where(block, jnp.concatenate([q] * heads, axis=0), 0.0).astype(jnp.bfloat16)
         top = jnp.full((tall, HEAD), NEG, jnp.float32)
         for i in range(steps):
-            if opening:
-                kl[i].wait()
             s = lax.dot_general(
                 q_block, kb[i * CHUNK : (i + 1) * CHUNK], NT, preferred_element_type=jnp.float32
             )
@@ -165,8 +206,6 @@
         peak = jnp.max(top, axis=1, keepdims=True)
         held = jnp.zeros((tall, HEAD), jnp.float32)
         for i in range(steps):
-            if opening:
-                vl[i].wait()
             s = sc[:, i * CHUNK : (i + 1) * CHUNK]
             e = jnp.where(s > 0.1 * NEG, jnp.exp(s - peak), 0.0)
             for j in range(CHUNK // HEAD):
@@ -197,23 +236,35 @@
         three = (rest - two.astype(jnp.float32)).astype(jnp.bfloat16)
         placed = (dot(put, one) + dot(put, two)) + dot(put, three)
         if opening:
-            part[...] = placed
+            put_all[...] = placed
         else:
-            part[...] += placed
+            put_all[...] += placed
 
     window(low, True)
     each(1, (high - low) // WIN + 1, lambda w: window(low + w * WIN, False))
-    stat = part[:, width:]
+    stat = put_all[:, width:]
     lanes = lax.broadcasted_iota(jnp.int32, stat.shape, 1)
-    part[:, width:] = jnp.where(
-        jnp.logical_and(lanes < heads, jnp.logical_not(here_s)), NEG, stat
-    )
+    stat = jnp.where(jnp.logical_and(lanes < heads, jnp.logical_not(here_s)), NEG, stat)
+    one = stat.astype(jnp.bfloat16).astype(jnp.float32)
+    two = (stat - one).astype(jnp.bfloat16).astype(jnp.float32)
+    three = (stat - one) - two
+    kinds = 2 * heads
+    stat = jnp.where(
+        lanes < kinds,
+        one,
+        jnp.where(
+            lanes < 2 * kinds, pltpu.roll(two, kinds, axis=1), pltpu.roll(three, 2 * kinds, axis=1)
+        ),
+    )
+    shape = part.shape
+    part[:, :, :width] = put_all[:, :width].reshape(shape[0], shape[1], width).astype(part.dtype)
+    part[:, :, width:] = stat.reshape(shape[0], shape[1], HEAD).astype(part.dtype)
 
 
 def tail(
-    n, t, nx, part, q_all, nk, nv, tok, gain, wo, up, down, hid,
-    got, wob, upb, dnb, zs, zr, mc, ns, nr, ts, rr,
-    lsem, a_s, a_r, u_s, u_r, d_s, d_r, z_s, z_r, n_s, n_r, r_s, r_r,
+    n, t, nx, part, q_all, nk, nv, tok, gain, wo, up, un, down, hid,
+    got, upb, dnb, zs, zr, mc, ns, nr, ts, rr,
+    lsem, a_s, a_r, u_s, u_r, d_s, d_r, e_s, e_r, z_s, z_r, n_s, n_r, r_s, r_r,
 ):
     me, z = lax.axis_index("req"), lax.axis_index("tp")
     ny = n // (2 * nx)
@@ -230,10 +281,10 @@
         return ((j // 2) * nx + x) * 2 + lax.rem(j, 2)
 
     loads = [
-        pltpu.make_async_copy(wo, wob, lsem.at[0]),
-        pltpu.make_async_copy(up, upb.at[x], lsem.at[1]),
-        pltpu.make_async_copy(down, dnb.at[x], lsem.at[2]),
+        pltpu.make_async_copy(up, upb.at[0], lsem.at[1]),
+        pltpu.make_async_copy(down, dnb.at[0], lsem.at[2]),
         pltpu.make_async_copy(part.at[me], got.at[me], lsem.at[3]),
+        pltpu.make_async_copy(un, upb.at[pl.ds(1, 2)], lsem.at[4]),
     ]
     for load in loads:
         load.start()
@@ -261,23 +312,6 @@
         )
 
     each(1, n, lambda d: partial_copy(d, me, lax.rem(me + d, n)).start())
-
-    def weight_copies(d, src):
-        peer = (y * nx + lax.rem(x + d, nx)) * 2 + c
-        return [
-            pltpu.make_async_remote_copy(
-                up, upb.at[src], u_s.at[d], u_r.at[src], device_id=(peer, z), device_id_type=MESH
-            ),
-            pltpu.make_async_remote_copy(
-                down, dnb.at[src], d_s.at[d], d_r.at[src], device_id=(peer, z), device_id_type=MESH
-            ),
-        ]
-
-    def weights_out(d):
-        for copy in weight_copies(d, x):
-            copy.start()
-
-    each(1, nx, weights_out)
 
     q = q_all[me].astype(jnp.float32)
     kn = nk[...].astype(jnp.float32)
@@ -287,7 +321,7 @@
     for h in range(heads):
         cols = slice(h * HEAD, (h + 1) * HEAD)
         mine = jnp.where(spot == h, jnp.sum(q[:, cols] * kn[:, cols], axis=1, keepdims=True), mine)
-    loads[3].wait()
+    loads[2].wait()
 
     def partial_in(d):
         copy = partial_copy(d, lax.rem(me + d, n), lax.rem(me + d, n))
@@ -295,7 +329,16 @@
         copy.wait_send()
 
     each(1, n, partial_in)
-    stat = got[:, :, width:]
+    down_side = side_copies(down, dnb.at[pl.ds(1, 2)], d_s, d_r, me, z, nx)
+    up_relay = relay_copies(un, upb.at[3], u_s, u_r, me, z, nx)
+    down_relay = relay_copies(dnb.at[pl.ds(1, 2)], dnb.at[3], e_s, e_r, me, z, nx)
+    for copy in down_side + up_relay:
+        copy.start()
+    kinds = 2 * heads
+    coded = got[:, :, width:].astype(jnp.float32)
+    stat = (coded + pltpu.roll(coded, HEAD - kinds, axis=2)) + pltpu.roll(
+        coded, HEAD - 2 * kinds, axis=2
+    )
     top = jnp.maximum(jnp.max(stat, axis=0), mine)
     scale = jnp.exp(stat - top[None])
     mass = pltpu.roll(stat, HEAD - heads, axis=2)
@@ -304,13 +347,11 @@
     pieces = []
     for h in range(heads):
         cols = slice(h * HEAD, (h + 1) * HEAD)
-        older = jnp.sum(got[:, :, cols] * scale[:, :, h : h + 1], axis=0)
+        older = jnp.sum(got[:, :, cols].astype(jnp.float32) * scale[:, :, h : h + 1], axis=0)
         pieces.append((self_w[:, h : h + 1] * vn[:, cols] + older) / total[:, h : h + 1])
     attended = jnp.concatenate(pieces, axis=1).astype(jnp.bfloat16)
-    loads[0].wait()
-    pm = dot(attended, wob[...])
-    zs[...] = pm
-    zr[z] = pm
+    pm = dot(attended, wo[...])
+    zs[...] = pm.astype(zs.dtype)
 
     def middle_copy(d, src):
         return pltpu.make_async_remote_copy(
@@ -326,10 +367,9 @@
         copy.wait_send()
 
     each(1, t, middle_in)
-    mid = zr[0]
     for i in range(1, t):
-        mid += zr[i]
-    mid += tok[...].astype(jnp.float32)
+        pm += zr[lax.rem(z + i, t)].astype(jnp.float32)
+    mid = tok[...].astype(jnp.float32) + pm
     for i in range(t):
         mc[i] = mid[:, i * width : (i + 1) * width]
     normed = norm(mid, gain[...]).astype(jnp.bfloat16)
@@ -343,6 +383,10 @@
         )
 
     each(1, nj, lambda d: normed_copy(d, j0).start())
+    for copy in down_side:
+        copy.wait()
+    for copy in down_relay:
+        copy.start()
 
     def normed_in(d):
         copy = normed_copy(d, lax.rem(j0 + d, nj))
@@ -350,25 +394,23 @@
         copy.wait_send()
 
     each(1, nj, normed_in)
-    loads[1].wait()
-    loads[2].wait()
-
-    def weights_in(d):
-        for copy in weight_copies(d, lax.rem(x + d, nx)):
-            copy.wait_recv()
-            copy.wait_send()
-
-    each(1, nx, weights_in)
+    loads[0].wait()
+    loads[3].wait()
+    for copy in up_relay:
+        copy.wait()
     tokens, units, wide = nj * own, nx * up.shape[0], up.shape[1]
     rows = nr[...].astype(jnp.float32).reshape(tokens, wide).astype(jnp.bfloat16)
     pre = lax.dot_general(
         rows, upb[...].reshape(units, wide), NT, preferred_element_type=jnp.float32
     )
     act = (0.5 * pre * (1.0 + lax.erf(pre * 0.5**0.5))).astype(jnp.bfloat16)
+    loads[1].wait()
+    for copy in down_relay:
+        copy.wait()
     for i in range(t):
         cols = slice(i * width, (i + 1) * width)
         term = dot(act, dnb[:, :, cols].reshape(units, width))
-        ts[:, i] = term.reshape(nj, own, width)
+        ts[:, i] = term.reshape(nj, own, width).astype(ts.dtype)
     rr[k0] = ts[j0, z]
 
     def term_copy(d, src):
@@ -386,7 +428,7 @@
         copy.wait_send()
 
     each(1, nk0, term_in)
-    hid[...] = (mc[z] + jnp.sum(rr[...], axis=0)).astype(jnp.bfloat16)
+    hid[...] = (mc[z] + jnp.sum(rr[...].astype(jnp.float32), axis=0)).astype(jnp.bfloat16)
 
 
 def body(
@@ -401,82 +443,101 @@
     rows = cache_keys.shape[0]
     steps = rows // CHUNK
     vmem = pl.BlockSpec(memory_space=pltpu.VMEM)
-    hbm = pl.BlockSpec(memory_space=pl.ANY)
+    hbm = pl.BlockSpec(memory_space=pltpu.HBM)
+    free = pl.BlockSpec(memory_space=pl.ANY)
     dma = pltpu.SemaphoreType.DMA
     shape = jax.ShapeDtypeStruct
-    q_all, nk, nv, tab = pl.pallas_call(
-        functools.partial(project, n),
+    up_rows = up_weight.T
+    held = lambda a: pltpu.with_memory_space_constraint(a, pltpu.HBM)
+    heads = width // HEAD
+    q_all, nk, nv, tab, kb, vb, un = pl.pallas_call(
+        functools.partial(project, n, nx),
         out_shape=(
             shape((n, own, width), b16),
             shape((own, width), b16),
             shape((own, width), b16),
             shape((8, requests), f32),
+            shape((rows, width), b16),
+            shape((rows, width), b16),
+            shape((2, units, wide), b16),
         ),
-        in_specs=[vmem] * 4 + [hbm] * 3,
-        out_specs=(vmem,) * 4,
+        in_specs=[hbm] * 10,
+        out_specs=(vmem,) * 7,
         scratch_shapes=[
+            pltpu.VMEM((own, wide), b16),
+            pltpu.VMEM((1, wide), f32),
+            pltpu.VMEM((1, requests), jnp.int32),
+            pltpu.VMEM((1, requests), jnp.int32),
             pltpu.VMEM((3, wide, width), b16),
             pltpu.VMEM((own, width), b16),
-            dma((6,)),
-            dma((n,)),
-            dma((n,)),
+            dma((12,)),
+            dma((n,)), dma((n,)),
+            dma((2,)), dma((2,)),
         ],
-        compiler_params=pltpu.CompilerParams(collective_id=0, has_side_effects=True),
+        compiler_params=pltpu.CompilerParams(
+            collective_id=0, has_side_effects=True, vmem_limit_bytes=VMEM_PROJECT
+        ),
         name="project",
     )(
-        tokens, first_gain.reshape(1, wide), lengths.reshape(1, requests),
-        stream_order.reshape(1, requests), query_weight, key_weight, value_weight,
+        *map(
+            held,
+            (
+                tokens, first_gain.reshape(1, wide), lengths.reshape(1, requests),
+                stream_order.reshape(1, requests), query_weight, key_weight, value_weight,
+                cache_keys, cache_values, up_rows,
+            ),
+        )
     )
     part, new_keys, new_values = pl.pallas_call(
         attend,
         out_shape=(
-            shape((requests, width + HEAD), f32),
+            shape((n, own, width + HEAD), b16),
             shape((own, width), b16),
             shape((own, width), b16),
         ),
-        in_specs=[vmem] * 4 + [hbm] * 2,
+        in_specs=[vmem] * 6,
         out_specs=(vmem,) * 3,
         scratch_shapes=[
-            pltpu.VMEM((rows, width), b16),
-            pltpu.VMEM((rows, width), b16),
-            pltpu.VMEM((WIN * width // HEAD, rows), f32),
-            pltpu.VMEM((WIN * width // HEAD, width), f32),
-            dma((steps,)),
-            dma((steps,)),
+            pltpu.VMEM((WIN * heads, rows), f32),
+            pltpu.VMEM((WIN * heads, width), f32),
+            pltpu.VMEM((requests, width + HEAD), f32),
         ],
+        compiler_params=pltpu.CompilerParams(vmem_limit_bytes=VMEM_ATTEND),
         name="attend",
-    )(q_all, tab, nk, nv, cache_keys, cache_values)
+    )(q_all, tab, nk, nv, kb, vb)
     nj = n // nx
     hidden = pl.pallas_call(
         functools.partial(tail, n, t, nx),
         out_shape=shape((own, width), b16),
-        in_specs=[hbm] + [vmem] * 5 + [hbm] * 3,
+        in_specs=[free] + [vmem] * 6 + [free, vmem, free],
         out_specs=vmem,
         scratch_shapes=[
-            pltpu.VMEM((n, own, width + HEAD), f32),
-            pltpu.VMEM((width, wide), b16),
+            pltpu.VMEM((n, own, width + HEAD), b16),
             pltpu.VMEM((nx, units, wide), b16),
             pltpu.VMEM((nx, units, wide), b16),
-            pltpu.VMEM((own, wide), f32),
-            pltpu.VMEM((t, own, wide), f32),
+            pltpu.VMEM((own, wide), b16),
+            pltpu.VMEM((t, own, wide), b16),
             pltpu.VMEM((t, own, width), f32),
             pltpu.VMEM((own, wide), b16),
             pltpu.VMEM((nj, own, wide), b16),
-            pltpu.VMEM((nj, t, own, width), f32),
-            pltpu.VMEM((nj * t, own, width), f32),
-            dma((4,)),
+            pltpu.VMEM((nj, t, own, width), b16),
+            pltpu.VMEM((nj * t, own, width), b16),
+            dma((5,)),
             dma((n,)), dma((n,)),
-            dma((nx,)), dma((nx,)),
-            dma((nx,)), dma((nx,)),
+            dma((2,)), dma((2,)),
+            dma((2,)), dma((2,)),
+            dma((2,)), dma((2,)),
             dma((t,)), dma((t,)),
             dma((nj,)), dma((nj,)),
             dma((nj * t,)), dma((nj * t,)),
         ],
-        compiler_params=pltpu.CompilerParams(collective_id=1, has_side_effects=True),
+        compiler_params=pltpu.CompilerParams(
+            collective_id=1, has_side_effects=True, vmem_limit_bytes=VMEM_TAIL
+        ),
         name="tail",
     )(
-        part.reshape(n, own, width + HEAD), q_all, new_keys, new_values, tokens,
-        second_gain.reshape(1, wide), out_weight, up_weight.T, down_weight,
+        part, q_all, nk, nv, tokens,
+        second_gain.reshape(1, wide), out_weight, up_rows, un, down_weight,
     )
     return hidden, new_keys, new_values
 

time: 75.7 us -> 58.7 us (0.78)
  Pallas kernels: 73.5 us -> 57.2 us
    pallas_call x1, Pallas kernels: 51.9 us -> 35.2 us  [body(): pl.pallas_call(functools.partial(tail, n, t, nx), out_shape=shape((own, w...]
where the time goes in v2:
time: 58.7 us; the launch traced here: 58.6 us
  Pallas kernels  57.2 us (97%)
  between operations  0.71 us (1%)
  local copies, waits for them, and re-layouts  0.63 us (1%)
    pallas_call x1, Pallas kernels, body(): pl.pallas_call(functools.partial(tail, n, t, nx), out_shape=shape((own, w...  35.2 us
    pallas_call x1, Pallas kernels, body(): pl.pallas_call(functools.partial(project, n, nx), out_shape=(shape((n, ow...  18.1 us
    pallas_call x1, Pallas kernels, body(): pl.pallas_call(attend, out_shape=(shape((n, own, width + HEAD), b16), sha...  3.92 us

profile of v2, /device:TPU:1, one launch (start us, length us, event | category | flops | bytes accessed | tf_op | source)
XLA Modules:
  0.0 58.6 jit_solution(5410590164037867232)
XLA Ops:
  0.6 18.1 %project.1 = (bf16[32,8,512]{2,1,0:T(8,128)(2,1)S(1)}, bf16[8,512]{1,0:T(8,128)(2,1)S(1)}, bf16[8,512]{1,0:T(8,128)(2,1)S(1)}, f32[8,256]{1,0:T(8,128)S(1)}, bf1...) custom-call(bf16[8,2048]{1,0:T(8,128)(2,1)} %tok.1, ...), custom_call_target="tpu_custom_call" | custom-call | tf_op jit(solution)/shard_map/project/pallas_call | solution.py:453
  18.7 0.0 copy-start
  18.7 0.0 copy-start.1
  18.7 0.0 copy-start.2
  18.8 0.0 copy-start.3
  18.8 0.0 copy-start.4
  18.8 3.9 %attend.1 = (bf16[32,8,640]{2,1,0:T(8,128)(2,1)S(1)}, bf16[8,512]{1,0:T(8,128)(2,1)}, bf16[8,512]{1,0:T(8,128)(2,1)}) custom-call(bf16[32,8,512]{2,1,0:T(8,128)(2,1)S(1)} %get-tuple-element.13.q_all, f32[8,256]{1,0:T(8,128)S(1)} %get-tuple-element.14.tab, bf16[8,512]{1,0:T(8,128)(2,1)S(1)} %get-tuple-element.15.nk_in.nk, ...), custom_call_target="tpu_custom_call" | custom-call | tf_op jit(solution)/shard_map/attend/pallas_call | solution.py:491
  22.7 0.0 copy-done
  22.7 0.0 copy-done.1
  22.7 0.0 copy-done.2
  22.7 0.0 copy-done.3
  22.7 0.0 copy-done.4
  22.7 35.2 %tail.1 = bf16[8,512]{1,0:T(8,128)(2,1)S(1)} custom-call(bf16[32,8,640]{2,1,0:T(8,128)(2,1)S(1)} %get-tuple-element.19.part, bf16[32,8,512]{2,1,0:T(8,128)(2,1)S(1)} %get-tuple-element.13.q_all, bf16[8,512]{1,0:T(8,128)(2,1)S(1)} %get-tuple-element.15.nk_in.nk, bf16[8,512]{1,0:T(8,128)(2,1)S(1)} %get-tuple-element.16.nv_in.nv, ...), custom_call_target="tpu_custom_call" | custom-call | tf_op jit(solution)/shard_map/tail/pallas_call | solution.py:509
  58.0 0.6 %copy.17 = bf16[8,512]{1,0:T(8,128)(2,1)} copy(bf16[8,512]{1,0:T(8,128)(2,1)S(1)} %tail.1) | data formatting | bytes 16384
Async XLA Ops:
  18.7 4.0 %copy-start = (bf16[512,2048]{1,0:T(8,128)(2,1)S(1)}, bf16[512,2048]{1,0:T(8,128)(2,1)}, u32[]{:S(2)}) copy-start(bf16[512,2048]{1,0:T(8,128)(2,1)} %wo.1) | copy-start | bytes 6291460
  18.7 4.0 %copy-start.1 = (bf16[2048,64]{0,1:T(8,128)(2,1)S(1)}, bf16[2048,64]{0,1:T(8,128)(2,1)}, u32[]{:S(2)}) copy-start(bf16[2048,64]{0,1:T(8,128)(2,1)} %param.20) | copy-start | bytes 786436
  18.7 4.0 %copy-start.2 = (bf16[64,2048]{1,0:T(8,128)(2,1)S(1)}, bf16[64,2048]{1,0:T(8,128)(2,1)}, u32[]{:S(2)}) copy-start(bf16[64,2048]{1,0:T(8,128)(2,1)} %down.1) | copy-start | bytes 786436
  18.8 4.0 %copy-start.3 = (bf16[8,2048]{1,0:T(8,128)(2,1)S(1)}, bf16[8,2048]{1,0:T(8,128)(2,1)}, u32[]{:S(2)}) copy-start(bf16[8,2048]{1,0:T(8,128)(2,1)} %tok.1) | copy-start | bytes 98308
  18.8 4.0 %copy-start.4 = (f32[2048]{0:T(1024)S(1)}, f32[2048]{0:T(1024)}, u32[]{:S(2)}) copy-start(f32[2048]{0:T(1024)} %param.19) | copy-start | bytes 24580

commit v3 on v2

--- a/solution.py
+++ b/solution.py
@@ -36,7 +36,7 @@
 
 
 def project(
-    n, nx, tok_h, gain_h, lens_h, order_h, wq, wk, wv, keys, values, up,
+    n, t, tok_h, gain_h, lens_h, order_h, wq, wk, wv, keys, values, up,
     q_all, nk, nv, tab, kb, vb, un,
     tok, gain, lens, order, wb, qs, wsem, ss, rs, us, ur,
 ):
@@ -67,6 +67,10 @@
         pl.semaphore_signal(barrier, inc=1, device_id=(peer, z), device_id_type=MESH)
 
     each(1, n, greet)
+    for d in (1, t - 1):
+        pl.semaphore_signal(
+            barrier, inc=1, device_id=(me, lax.rem(z + d, t)), device_id_type=MESH
+        )
     small[0].wait()
     small[1].wait()
     normed = norm(tok[...].astype(jnp.float32), gain[...]).astype(jnp.bfloat16)
@@ -79,7 +83,7 @@
     q = (q * HEAD**-0.5).astype(jnp.bfloat16)
     qs[...] = q
     q_all[me] = q
-    pl.semaphore_wait(barrier, n - 1)
+    pl.semaphore_wait(barrier, n + 1)
 
     def send(d):
         peer = lax.rem(me + d, n)
@@ -88,7 +92,7 @@
         ).start()
 
     each(1, n, send)
-    sides = side_copies(up, un, us, ur, me, z, nx)
+    sides = side_copies(up, un, us, ur, me, z, t)
     for copy in sides:
         copy.start()
     loads[4].wait()
@@ -128,29 +132,24 @@
         copy.wait()
 
 
-def along(me, d, nx):
-    x = lax.rem(me // 2, nx)
-    return me + (lax.rem(x + d, nx) - x) * 2
-
-
-def side_copies(src, dst, ss, rs, me, z, nx):
+def side_copies(src, dst, ss, rs, me, z, t):
     return [
         pltpu.make_async_remote_copy(
             src, dst.at[i], ss.at[i], rs.at[i],
-            device_id=(along(me, d, nx), z), device_id_type=MESH,
-        )
-        for i, d in enumerate((1, nx - 1))
+            device_id=(me, lax.rem(z + d, t)), device_id_type=MESH,
+        )
+        for i, d in enumerate((1, t - 1))
     ]
 
 
-def relay_copies(slots, dst, ss, rs, me, z, nx):
+def relay_copies(slots, dst, ss, rs, me, z, t):
     half = dst.shape[0] // 2
     return [
         pltpu.make_async_remote_copy(
             slots.at[i, pl.ds(i * half, half)], dst.at[pl.ds(i * half, half)], ss.at[i], rs.at[i],
-            device_id=(along(me, d, nx), z), device_id_type=MESH,
-        )
-        for i, d in enumerate((1, nx - 1))
+            device_id=(me, lax.rem(z + d, t)), device_id_type=MESH,
+        )
+        for i, d in enumerate((1, t - 1))
     ]
 
 
@@ -262,29 +261,21 @@
 
 
 def tail(
-    n, t, nx, part, q_all, nk, nv, tok, gain, wo, up, un, down, hid,
-    got, upb, dnb, zs, zr, mc, ns, nr, ts, rr,
-    lsem, a_s, a_r, u_s, u_r, d_s, d_r, e_s, e_r, z_s, z_r, n_s, n_r, r_s, r_r,
+    n, t, part, q_all, nk, nv, tok, gain, wo, up, un, down, hid,
+    got, upb, dnb, zs, zr, tp, ns, nr, ts, rr, fs, fr,
+    lsem, a_s, a_r, u_s, u_r, d_s, d_r, e_s, e_r, z_s, z_r, n_s, n_r, r_s, r_r, f_s, f_r,
 ):
     me, z = lax.axis_index("req"), lax.axis_index("tp")
-    ny = n // (2 * nx)
-    y, x, c = me // (2 * nx), lax.rem(me // 2, nx), lax.rem(me, 2)
-    nj = 2 * ny
-    j0 = y * 2 + c
-    k0 = j0 * t + z
-    nk0 = nj * t
+    f32, b16 = jnp.float32, jnp.bfloat16
     width = q_all.shape[2]
     heads = width // HEAD
-    own = tok.shape[0]
-
-    def home(j):
-        return ((j // 2) * nx + x) * 2 + lax.rem(j, 2)
-
+    own, wide = tok.shape
+    few = own // t
     loads = [
-        pltpu.make_async_copy(up, upb.at[0], lsem.at[1]),
-        pltpu.make_async_copy(down, dnb.at[0], lsem.at[2]),
-        pltpu.make_async_copy(part.at[me], got.at[me], lsem.at[3]),
-        pltpu.make_async_copy(un, upb.at[pl.ds(1, 2)], lsem.at[4]),
+        pltpu.make_async_copy(up, upb.at[0], lsem.at[0]),
+        pltpu.make_async_copy(down, dnb.at[0], lsem.at[1]),
+        pltpu.make_async_copy(part.at[me], got.at[me], lsem.at[2]),
+        pltpu.make_async_copy(un, upb.at[pl.ds(1, 2)], lsem.at[3]),
     ]
     for load in loads:
         load.start()
@@ -296,46 +287,91 @@
 
     each(1, n, greet)
 
-    def greet_plane(i):
-        pz = lax.rem(z + 1 + i // nj, t)
+    def greet_z(d):
         pl.semaphore_signal(
-            barrier, inc=1, device_id=(home(lax.rem(i, nj)), pz), device_id_type=MESH
-        )
-
-    each(0, nj * (t - 1), greet_plane)
-    pl.semaphore_wait(barrier, n - 1 + nj * (t - 1))
-
-    def partial_copy(d, src, peer):
-        return pltpu.make_async_remote_copy(
-            part.at[peer], got.at[src], a_s.at[d], a_r.at[src],
-            device_id=(peer, z), device_id_type=MESH,
-        )
-
-    each(1, n, lambda d: partial_copy(d, me, lax.rem(me + d, n)).start())
-
-    q = q_all[me].astype(jnp.float32)
-    kn = nk[...].astype(jnp.float32)
-    vn = nv[...].astype(jnp.float32)
+            barrier, inc=1, device_id=(me, lax.rem(z + d, t)), device_id_type=MESH
+        )
+
+    each(1, t, greet_z)
+    pl.semaphore_wait(barrier, n - 1 + t - 1)
+
+    def line_copies(src, dst, ss, rs):
+        def one(d, s, peer):
+            return pltpu.make_async_remote_copy(
+                src(peer), dst.at[s], ss.at[d], rs.at[s], device_id=(peer, z), device_id_type=MESH
+            )
+
+        def start():
+            each(1, n, lambda d: one(d, me, lax.rem(me + d, n)).start())
+
+        def finish():
+            def wait(d):
+                other = lax.rem(me + d, n)
+                copy = one(d, other, other)
+                copy.wait_recv()
+                copy.wait_send()
+
+            each(1, n, wait)
+
+        return start, finish
+
+    def z_copies(src, dst, ss, rs):
+        def one(d, s):
+            peer = lax.rem(z + d, t)
+            return pltpu.make_async_remote_copy(
+                src(peer), dst.at[s], ss.at[d], rs.at[s], device_id=(me, peer), device_id_type=MESH
+            )
+
+        def start():
+            each(1, t, lambda d: one(d, z).start())
+
+        def finish():
+            def wait(d):
+                copy = one(d, lax.rem(z + d, t))
+                copy.wait_recv()
+                copy.wait_send()
+
+            each(1, t, wait)
+
+        return start, finish
+
+    send, take = line_copies(lambda peer: part.at[peer], got, a_s, a_r)
+    send()
+    sides = dnb.at[pl.ds(1, 2)]
+    up_relay = relay_copies(un, upb.at[t - 1], u_s, u_r, me, z, t)
+    down_side = side_copies(down, sides, d_s, d_r, me, z, t)
+    down_relay = relay_copies(sides, dnb.at[t - 1], e_s, e_r, me, z, t)
+    for copy in up_relay + down_side:
+        copy.start()
+
+    def pieces(a):
+        return [
+            jnp.concatenate(
+                [a[k * few : (k + 1) * few, b * width : (b + 1) * width] for b in range(t)], axis=0
+            )
+            for k in range(t)
+        ]
+
+    q = q_all[me].astype(f32)
+    kn = nk[...].astype(f32)
+    vn = nv[...].astype(f32)
     spot = lax.broadcasted_iota(jnp.int32, (own, HEAD), 1)
-    mine = jnp.zeros((own, HEAD), jnp.float32)
+    mine = jnp.zeros((own, HEAD), f32)
     for h in range(heads):
         cols = slice(h * HEAD, (h + 1) * HEAD)
         mine = jnp.where(spot == h, jnp.sum(q[:, cols] * kn[:, cols], axis=1, keepdims=True), mine)
+    for k, piece in enumerate(pieces(tok[...].astype(f32))):
+        tp[k] = piece
+    gains = jnp.concatenate(
+        [
+            jnp.broadcast_to(gain[:, b * width : (b + 1) * width], (few, width)) for b in range(t)
+        ],
+        axis=0,
+    )
     loads[2].wait()
-
-    def partial_in(d):
-        copy = partial_copy(d, lax.rem(me + d, n), lax.rem(me + d, n))
-        copy.wait_recv()
-        copy.wait_send()
-
-    each(1, n, partial_in)
-    down_side = side_copies(down, dnb.at[pl.ds(1, 2)], d_s, d_r, me, z, nx)
-    up_relay = relay_copies(un, upb.at[3], u_s, u_r, me, z, nx)
-    down_relay = relay_copies(dnb.at[pl.ds(1, 2)], dnb.at[3], e_s, e_r, me, z, nx)
-    for copy in down_side + up_relay:
-        copy.start()
+    take()
     kinds = 2 * heads
-    coded = got[:, :, width:].astype(jnp.float32)
+    coded = got[:, :, width:].astype(f32)
     stat = (coded + pltpu.roll(coded, HEAD - kinds, axis=2)) + pltpu.roll(
         coded, HEAD - 2 * kinds, axis=2
     )
@@ -344,95 +380,88 @@
     mass = pltpu.roll(stat, HEAD - heads, axis=2)
     self_w = jnp.exp(mine - top)
     total = self_w + jnp.sum(scale * mass, axis=0)
-    pieces = []
+    attended = []
     for h in range(heads):
         cols = slice(h * HEAD, (h + 1) * HEAD)
-        older = jnp.sum(got[:, :, cols].astype(jnp.float32) * scale[:, :, h : h + 1], axis=0)
-        pieces.append((self_w[:, h : h + 1] * vn[:, cols] + older) / total[:, h : h + 1])
-    attended = jnp.concatenate(pieces, axis=1).astype(jnp.bfloat16)
-    pm = dot(attended, wo[...])
-    zs[...] = pm.astype(zs.dtype)
-
-    def middle_copy(d, src):
-        return pltpu.make_async_remote_copy(
-            zs, zr.at[src], z_s.at[d], z_r.at[src],
-            device_id=(me, lax.rem(z + d, t)), device_id_type=MESH,
-        )
-
-    each(1, t, lambda d: middle_copy(d, z).start())
-
-    def middle_in(d):
-        copy = middle_copy(d, lax.rem(z + d, t))
-        copy.wait_recv()
-        copy.wait_send()
-
-    each(1, t, middle_in)
+        older = jnp.sum(got[:, :, cols].astype(f32) * scale[:, :, h : h + 1], axis=0)
+        attended.append((self_w[:, h : h + 1] * vn[:, cols] + older) / total[:, h : h + 1])
+    attended = jnp.concatenate(attended, axis=1).astype(b16)
+    for k, piece in enumerate(pieces(dot(attended, wo[...]))):
+        zs[k] = piece
+    send, take = z_copies(lambda peer: zs.at[peer], zr, z_s, z_r)
+    send()
+    mid = zs[z]
+    take()
     for i in range(1, t):
-        pm += zr[lax.rem(z + i, t)].astype(jnp.float32)
-    mid = tok[...].astype(jnp.float32) + pm
-    for i in range(t):
-        mc[i] = mid[:, i * width : (i + 1) * width]
-    normed = norm(mid, gain[...]).astype(jnp.bfloat16)
-    ns[...] = normed
-    nr[j0] = normed
-
-    def normed_copy(d, src):
-        return pltpu.make_async_remote_copy(
-            ns, nr.at[src], n_s.at[d], n_r.at[src],
-            device_id=(home(lax.rem(j0 + d, nj)), z), device_id_type=MESH,
-        )
-
-    each(1, nj, lambda d: normed_copy(d, j0).start())
+        mid += zr[lax.rem(z + i, t)]
+    mid += tp[z]
     for copy in down_side:
         copy.wait()
     for copy in down_relay:
         copy.start()
 
-    def normed_in(d):
-        copy = normed_copy(d, lax.rem(j0 + d, nj))
-        copy.wait_recv()
-        copy.wait_send()
-
-    each(1, nj, normed_in)
+    def mean(a):
+        r = jnp.broadcast_to(jnp.sum(a, axis=1, keepdims=True), (own, HEAD))
+        whole = r
+        for b in range(1, t):
+            whole += pltpu.roll(r, b * few, axis=0)
+        return whole[:, :1] / wide
+
+    shifted = mid - mean(mid)
+    normed = (shifted * lax.rsqrt(mean(shifted * shifted) + 1e-05) * gains).astype(b16)
+    ns[...] = normed
+    nr[me] = normed
+    send, take = line_copies(lambda peer: ns, nr, n_s, n_r)
+    send()
     loads[0].wait()
     loads[3].wait()
     for copy in up_relay:
         copy.wait()
-    tokens, units, wide = nj * own, nx * up.shape[0], up.shape[1]
-    rows = nr[...].astype(jnp.float32).reshape(tokens, wide).astype(jnp.bfloat16)
-    pre = lax.dot_general(
-        rows, upb[...].reshape(units, wide), NT, preferred_element_type=jnp.float32
-    )
-    act = (0.5 * pre * (1.0 + lax.erf(pre * 0.5**0.5))).astype(jnp.bfloat16)
+    take()
+    rows, units = n * own, t * up.shape[0]
+    row_block = lax.rem(lax.broadcasted_iota(jnp.int32, (rows, width), 0), own) // few
+    x = nr[...].astype(f32).reshape(rows, width).astype(b16)
+    pre = jnp.zeros((rows, units), f32)
+    for b in range(t):
+        y = lax.dot_general(
+            x, upb[:, :, b * width : (b + 1) * width].reshape(units, width), NT,
+            preferred_element_type=f32,
+        )
+        pre = jnp.where(row_block[:, :units] == b, y, pre)
+    pre = pre.reshape(n, own, units)
+    whole = pre
+    for b in range(1, t):
+        whole += pltpu.roll(pre, b * few, axis=1)
+    act = (0.5 * whole * (1.0 + lax.erf(whole * 0.5**0.5))).reshape(rows, units).astype(b16)
     loads[1].wait()
     for copy in down_relay:
         copy.wait()
-    for i in range(t):
-        cols = slice(i * width, (i + 1) * width)
-        term = dot(act, dnb[:, :, cols].reshape(units, width))
-        ts[:, i] = term.reshape(nj, own, width).astype(ts.dtype)
-    rr[k0] = ts[j0, z]
-
-    def term_copy(d, src):
-        k = lax.rem(k0 + d, nk0)
-        return pltpu.make_async_remote_copy(
-            ts.at[k // t, lax.rem(k, t)], rr.at[src], r_s.at[d], r_r.at[src],
-            device_id=(home(k // t), lax.rem(k, t)), device_id_type=MESH,
-        )
-
-    each(1, nk0, lambda d: term_copy(d, k0).start())
-
-    def term_in(d):
-        copy = term_copy(d, lax.rem(k0 + d, nk0))
-        copy.wait_recv()
-        copy.wait_send()
-
-    each(1, nk0, term_in)
-    hid[...] = (mc[z] + jnp.sum(rr[...].astype(jnp.float32), axis=0)).astype(jnp.bfloat16)
+    term = jnp.zeros((rows, width), f32)
+    for b in range(t):
+        y = dot(act, dnb[:, :, b * width : (b + 1) * width].reshape(units, width))
+        term = jnp.where(row_block == b, y, term)
+    term = term.reshape(n, own, width).astype(b16)
+    ts[...] = term
+    send, take = line_copies(lambda peer: ts.at[peer], rr, r_s, r_r)
+    send()
+    rr[me] = ts[me]
+    take()
+    out = (mid + jnp.sum(rr[...].astype(f32), axis=0)).astype(b16)
+    fs[...] = out
+    fr[z] = out
+    send, take = z_copies(lambda peer: fs, fr, f_s, f_r)
+    send()
+    take()
+    every = [fr[k].astype(f32) for k in range(t)]
+    final = jnp.zeros((own, width), f32)
+    for b in range(t):
+        rows_b = jnp.concatenate([a[b * few : (b + 1) * few] for a in every], axis=0)
+        final = jnp.where(z == b, rows_b, final)
+    hid[...] = final.astype(b16)
 
 
 def body(
-    n, t, nx, tokens, first_gain, query_weight, key_weight, value_weight, out_weight, second_gain,
+    n, t, tokens, first_gain, query_weight, key_weight, value_weight, out_weight, second_gain,
     up_weight, down_weight, cache_keys, cache_values, lengths, stream_order,
 ):
     f32, b16 = jnp.float32, jnp.bfloat16
@@ -451,7 +480,7 @@
     held = lambda a: pltpu.with_memory_space_constraint(a, pltpu.HBM)
     heads = width // HEAD
     q_all, nk, nv, tab, kb, vb, un = pl.pallas_call(
-        functools.partial(project, n, nx),
+        functools.partial(project, n, t),
         out_shape=(
             shape((n, own, width), b16),
             shape((own, width), b16),
@@ -505,31 +534,33 @@
         compiler_params=pltpu.CompilerParams(vmem_limit_bytes=VMEM_ATTEND),
         name="attend",
     )(q_all, tab, nk, nv, kb, vb)
-    nj = n // nx
     hidden = pl.pallas_call(
-        functools.partial(tail, n, t, nx),
+        functools.partial(tail, n, t),
         out_shape=shape((own, width), b16),
         in_specs=[free] + [vmem] * 6 + [free, vmem, free],
         out_specs=vmem,
         scratch_shapes=[
             pltpu.VMEM((n, own, width + HEAD), b16),
-            pltpu.VMEM((nx, units, wide), b16),
-            pltpu.VMEM((nx, units, wide), b16),
-            pltpu.VMEM((own, wide), b16),
-            pltpu.VMEM((t, own, wide), b16),
+            pltpu.VMEM((t, units, wide), b16),
+            pltpu.VMEM((t, units, wide), b16),
             pltpu.VMEM((t, own, width), f32),
-            pltpu.VMEM((own, wide), b16),
-            pltpu.VMEM((nj, own, wide), b16),
-            pltpu.VMEM((nj, t, own, width), b16),
-            pltpu.VMEM((nj * t, own, width), b16),
-            dma((5,)),
+            pltpu.VMEM((t, own, width), f32),
+            pltpu.VMEM((t, own, width), f32),
+            pltpu.VMEM((own, width), b16),
+            pltpu.VMEM((n, own, width), b16),
+            pltpu.VMEM((n, own, width), b16),
+            pltpu.VMEM((n, own, width), b16),
+            pltpu.VMEM((own, width), b16),
+            pltpu.VMEM((t, own, width), b16),
+            dma((4,)),
             dma((n,)), dma((n,)),
             dma((2,)), dma((2,)),
             dma((2,)), dma((2,)),
             dma((2,)), dma((2,)),
             dma((t,)), dma((t,)),
-            dma((nj,)), dma((nj,)),
-            dma((nj * t,)), dma((nj * t,)),
+            dma((n,)), dma((n,)),
+            dma((n,)), dma((n,)),
+            dma((t,)), dma((t,)),
         ],
         compiler_params=pltpu.CompilerParams(
             collective_id=1, has_side_effects=True, vmem_limit_bytes=VMEM_TAIL
@@ -545,7 +576,7 @@
 def solution(mesh):
     n, t = mesh.shape["req"], mesh.shape["tp"]
     return jax.shard_map(
-        functools.partial(body, n, t, 4),
+        functools.partial(body, n, t),
         mesh=mesh,
         in_specs=(
             P("req", None), P(), P(None, "tp"), P(None, "tp"), P(None, "tp"), P("tp", None), P(),

time: 58.7 us -> 56.5 us (0.963)
  Pallas kernels: 57.2 us -> 55.1 us
    pallas_call x2, Pallas kernels: 53.3 us -> 51.1 us  [the longest x1 32.9 us: body(): pl.pallas_call(functools.partial(tail, n, t), out_shape=shape((own, width...]
where the time goes in v3:
time: 56.5 us; the launch traced here: 56.4 us
  Pallas kernels  55.1 us (98%)
  between operations  0.71 us (1%)
  local copies, waits for them, and re-layouts  0.63 us (1%)
    pallas_call x1, Pallas kernels, body(): pl.pallas_call(functools.partial(tail, n, t), out_shape=shape((own, width...  32.9 us
    pallas_call x1, Pallas kernels, body(): pl.pallas_call(functools.partial(project, n, t), out_shape=(shape((n, own...  18.2 us
    pallas_call x1, Pallas kernels, body(): pl.pallas_call(attend, out_shape=(shape((n, own, width + HEAD), b16), sha...  3.92 us

profile of v3, /device:TPU:1, one launch (start us, length us, event | category | flops | bytes accessed | tf_op | source)
XLA Modules:
  0.0 56.4 jit_solution(10639393202662641607)
XLA Ops:
  0.6 18.2 %project.1 = (bf16[32,8,512]{2,1,0:T(8,128)(2,1)S(1)}, bf16[8,512]{1,0:T(8,128)(2,1)S(1)}, bf16[8,512]{1,0:T(8,128)(2,1)S(1)}, f32[8,256]{1,0:T(8,128)S(1)}, bf1...) custom-call(bf16[8,2048]{1,0:T(8,128)(2,1)} %tok.1, ...), custom_call_target="tpu_custom_call" | custom-call | tf_op jit(solution)/shard_map/project/pallas_call | solution.py:482
  18.8 0.0 copy-start
  18.9 0.0 copy-start.1
  18.9 0.0 copy-start.2
  18.9 0.0 copy-start.3
  18.9 0.0 copy-start.4
  18.9 3.9 %attend.1 = (bf16[32,8,640]{2,1,0:T(8,128)(2,1)S(1)}, bf16[8,512]{1,0:T(8,128)(2,1)}, bf16[8,512]{1,0:T(8,128)(2,1)}) custom-call(bf16[32,8,512]{2,1,0:T(8,128)(2,1)S(1)} %get-tuple-element.13.q_all, f32[8,256]{1,0:T(8,128)S(1)} %get-tuple-element.14.tab, bf16[8,512]{1,0:T(8,128)(2,1)S(1)} %get-tuple-element.15.nk_in.nk, ...), custom_call_target="tpu_custom_call" | custom-call | tf_op jit(solution)/shard_map/attend/pallas_call | solution.py:520
  22.8 0.0 copy-done
  22.8 0.0 copy-done.1
  22.8 0.0 copy-done.2
  22.8 0.0 copy-done.3
  22.8 0.0 copy-done.4
  22.9 32.9 %tail.1 = bf16[8,512]{1,0:T(8,128)(2,1)S(1)} custom-call(bf16[32,8,640]{2,1,0:T(8,128)(2,1)S(1)} %get-tuple-element.19.part, bf16[32,8,512]{2,1,0:T(8,128)(2,1)S(1)} %get-tuple-element.13.q_all, bf16[8,512]{1,0:T(8,128)(2,1)S(1)} %get-tuple-element.15.nk_in.nk, bf16[8,512]{1,0:T(8,128)(2,1)S(1)} %get-tuple-element.16.nv_in.nv, ...), custom_call_target="tpu_custom_call" | custom-call | tf_op jit(solution)/shard_map/tail/pallas_call | solution.py:537
  55.8 0.6 %copy.17 = bf16[8,512]{1,0:T(8,128)(2,1)} copy(bf16[8,512]{1,0:T(8,128)(2,1)S(1)} %tail.1) | data formatting | bytes 16384
Async XLA Ops:
  18.8 4.0 %copy-start = (bf16[512,2048]{1,0:T(8,128)(2,1)S(1)}, bf16[512,2048]{1,0:T(8,128)(2,1)}, u32[]{:S(2)}) copy-start(bf16[512,2048]{1,0:T(8,128)(2,1)} %wo.1) | copy-start | bytes 6291460
  18.9 4.0 %copy-start.1 = (bf16[2048,64]{0,1:T(8,128)(2,1)S(1)}, bf16[2048,64]{0,1:T(8,128)(2,1)}, u32[]{:S(2)}) copy-start(bf16[2048,64]{0,1:T(8,128)(2,1)} %param.20) | copy-start | bytes 786436
  18.9 4.0 %copy-start.2 = (bf16[64,2048]{1,0:T(8,128)(2,1)S(1)}, bf16[64,2048]{1,0:T(8,128)(2,1)}, u32[]{:S(2)}) copy-start(bf16[64,2048]{1,0:T(8,128)(2,1)} %down.1) | copy-start | bytes 786436
  18.9 4.0 %copy-start.3 = (bf16[8,2048]{1,0:T(8,128)(2,1)S(1)}, bf16[8,2048]{1,0:T(8,128)(2,1)}, u32[]{:S(2)}) copy-start(bf16[8,2048]{1,0:T(8,128)(2,1)} %tok.1) | copy-start | bytes 98308
  18.9 4.0 %copy-start.4 = (f32[2048]{0:T(1024)S(1)}, f32[2048]{0:T(1024)}, u32[]{:S(2)}) copy-start(f32[2048]{0:T(1024)} %param.19) | copy-start | bytes 24580

commit v4 on v3

--- a/solution.py
+++ b/solution.py
@@ -1,4 +1,5 @@
 import functools
+import math
 
 import jax
 import jax.numpy as jnp
@@ -33,6 +34,23 @@
         return carry
 
     lax.fori_loop(lo, hi, step, 0)
+
+
+def line(n, me):
+    side = math.isqrt(n // 2)
+    y, x, c = me // (2 * side), lax.rem(me // 2, side), lax.rem(me, 2)
+    far = lambda o: min(o[0], side - o[0]) + min(o[1], side - o[1])
+    steps = [(i, j, k) for i in range(side) for j in range(side) for k in range(2)]
+    steps = sorted(steps[1:], key=lambda o: (-far(o), -o[2]))
+    ys = [lax.rem(y + i, side) for i in range(side)]
+    xs = [lax.rem(x + i, side) for i in range(side)]
+    cs = [c, 1 - c]
+    return [(i, (ys[a] * side + xs[b]) * 2 + cs[k]) for i, (a, b, k) in enumerate(steps)]
+
+
+def ring(t, z):
+    steps = sorted(range(1, t), key=lambda d: -min(d, t - d))
+    return [(d, lax.rem(z + d, t)) for d in steps]
 
 
 def project(
@@ -62,11 +80,9 @@
         load.start()
     barrier = pltpu.get_barrier_semaphore()
 
-    def greet(d):
-        peer = lax.rem(me + d, n)
+    others = line(n, me)
+    for _, peer in others:
         pl.semaphore_signal(barrier, inc=1, device_id=(peer, z), device_id_type=MESH)
-
-    each(1, n, greet)
     for d in (1, t - 1):
         pl.semaphore_signal(
             barrier, inc=1, device_id=(me, lax.rem(z + d, t)), device_id_type=MESH
@@ -74,6 +90,10 @@
     small[0].wait()
     small[1].wait()
     normed = norm(tok[...].astype(jnp.float32), gain[...]).astype(jnp.bfloat16)
+    pl.semaphore_wait(barrier, n + 1)
+    sides = side_copies(up, un, us, ur, me, z, t)
+    for copy in sides:
+        copy.start()
     q = jnp.zeros((tok.shape[0], wq.shape[1]), jnp.float32)
     for i in range(4):
         loads[i].wait()
@@ -83,18 +103,10 @@
     q = (q * HEAD**-0.5).astype(jnp.bfloat16)
     qs[...] = q
     q_all[me] = q
-    pl.semaphore_wait(barrier, n + 1)
-
-    def send(d):
-        peer = lax.rem(me + d, n)
+    for i, peer in others:
         pltpu.make_async_remote_copy(
-            qs, q_all.at[me], ss.at[d], rs.at[me], device_id=(peer, z), device_id_type=MESH
+            qs, q_all.at[me], ss.at[i], rs.at[me], device_id=(peer, z), device_id_type=MESH
         ).start()
-
-    each(1, n, send)
-    sides = side_copies(up, un, us, ur, me, z, t)
-    for copy in sides:
-        copy.start()
     loads[4].wait()
     nk[...] = dot(normed, wb[1]).astype(jnp.bfloat16)
     loads[5].wait()
@@ -117,15 +129,12 @@
     tab[2:3] = end
     tab[3:8] = jnp.zeros((5, m), jnp.float32)
 
-    def finish(d):
-        src = lax.rem(me + d, n)
+    for i, src in others:
         copy = pltpu.make_async_remote_copy(
-            qs, q_all.at[src], ss.at[d], rs.at[src], device_id=(src, z), device_id_type=MESH
+            qs, q_all.at[src], ss.at[i], rs.at[src], device_id=(src, z), device_id_type=MESH
         )
         copy.wait_recv()
         copy.wait_send()
-
-    each(1, n, finish)
     loads[6].wait()
     loads[7].wait()
     for copy in sides:
@@ -281,18 +290,11 @@
         load.start()
     barrier = pltpu.get_barrier_semaphore()
 
-    def greet(d):
-        peer = lax.rem(me + d, n)
+    others, others_z = line(n, me), ring(t, z)
+    for _, peer in others:
         pl.semaphore_signal(barrier, inc=1, device_id=(peer, z), device_id_type=MESH)
-
-    each(1, n, greet)
-
-    def greet_z(d):
-        pl.semaphore_signal(
-            barrier, inc=1, device_id=(me, lax.rem(z + d, t)), device_id_type=MESH
-        )
-
-    each(1, t, greet_z)
+    for _, peer in others_z:
+        pl.semaphore_signal(barrier, inc=1, device_id=(me, peer), device_id_type=MESH)
     pl.semaphore_wait(barrier, n - 1 + t - 1)
 
     def line_copies(src, dst, ss, rs):
@@ -302,36 +304,32 @@
             )
 
         def start():
-            each(1, n, lambda d: one(d, me, lax.rem(me + d, n)).start())
+            for i, peer in others:
+                one(i, me, peer).start()
 
         def finish():
-            def wait(d):
-                other = lax.rem(me + d, n)
-                copy = one(d, other, other)
+            for i, peer in others:
+                copy = one(i, peer, peer)
                 copy.wait_recv()
                 copy.wait_send()
 
-            each(1, n, wait)
-
         return start, finish
 
     def z_copies(src, dst, ss, rs):
-        def one(d, s):
-            peer = lax.rem(z + d, t)
+        def one(d, s, peer):
             return pltpu.make_async_remote_copy(
                 src(peer), dst.at[s], ss.at[d], rs.at[s], device_id=(me, peer), device_id_type=MESH
             )
 
         def start():
-            each(1, t, lambda d: one(d, z).start())
+            for d, peer in others_z:
+                one(d, z, peer).start()
 
         def finish():
-            def wait(d):
-                copy = one(d, lax.rem(z + d, t))
+            for d, peer in others_z:
+                copy = one(d, peer, peer)
                 copy.wait_recv()
                 copy.wait_send()
-
-            each(1, t, wait)
 
         return start, finish
 

time: 56.5 us -> 55.1 us (0.975)
  Pallas kernels: 55.1 us -> 53.5 us
    pallas_call x1, Pallas kernels: 32.9 us -> 31.7 us  [body(): pl.pallas_call(functools.partial(tail, n, t), out_shape=shape((own, width...]
where the time goes in v4:
time: 55.1 us; the launch traced here: 54.8 us
  Pallas kernels  53.5 us (97%)
  between operations  0.71 us (1%)
  local copies, waits for them, and re-layouts  0.63 us (1%)
    pallas_call x1, Pallas kernels, body(): pl.pallas_call(functools.partial(tail, n, t), out_shape=shape((own, width...  31.7 us
    pallas_call x1, Pallas kernels, body(): pl.pallas_call(functools.partial(project, n, t), out_shape=(shape((n, own...  17.9 us
    pallas_call x1, Pallas kernels, body(): pl.pallas_call(attend, out_shape=(shape((n, own, width + HEAD), b16), sha...  3.92 us

profile of v4, /device:TPU:1, one launch (start us, length us, event | category | flops | bytes accessed | tf_op | source)
XLA Modules:
  0.0 54.8 jit_solution(8170517467354332934)
XLA Ops:
  0.6 17.9 %project.1 = (bf16[32,8,512]{2,1,0:T(8,128)(2,1)S(1)}, bf16[8,512]{1,0:T(8,128)(2,1)S(1)}, bf16[8,512]{1,0:T(8,128)(2,1)S(1)}, f32[8,256]{1,0:T(8,128)S(1)}, bf1...) custom-call(bf16[8,2048]{1,0:T(8,128)(2,1)} %tok.1, ...), custom_call_target="tpu_custom_call" | custom-call | tf_op jit(solution)/shard_map/project/pallas_call | solution.py:480
  18.5 0.0 copy-start
  18.5 0.0 copy-start.1
  18.5 0.0 copy-start.2
  18.5 0.0 copy-start.3
  18.5 0.0 copy-start.4
  18.6 3.9 %attend.1 = (bf16[32,8,640]{2,1,0:T(8,128)(2,1)S(1)}, bf16[8,512]{1,0:T(8,128)(2,1)}, bf16[8,512]{1,0:T(8,128)(2,1)}) custom-call(bf16[32,8,512]{2,1,0:T(8,128)(2,1)S(1)} %get-tuple-element.13.q_all, f32[8,256]{1,0:T(8,128)S(1)} %get-tuple-element.14.tab, bf16[8,512]{1,0:T(8,128)(2,1)S(1)} %get-tuple-element.15.nk_in.nk, ...), custom_call_target="tpu_custom_call" | custom-call | tf_op jit(solution)/shard_map/attend/pallas_call | solution.py:518
  22.5 0.0 copy-done
  22.5 0.0 copy-done.1
  22.5 0.0 copy-done.2
  22.5 0.0 copy-done.3
  22.5 0.0 copy-done.4
  22.5 31.7 %tail.1 = bf16[8,512]{1,0:T(8,128)(2,1)S(1)} custom-call(bf16[32,8,640]{2,1,0:T(8,128)(2,1)S(1)} %get-tuple-element.19.part, bf16[32,8,512]{2,1,0:T(8,128)(2,1)S(1)} %get-tuple-element.13.q_all, bf16[8,512]{1,0:T(8,128)(2,1)S(1)} %get-tuple-element.15.nk_in.nk, bf16[8,512]{1,0:T(8,128)(2,1)S(1)} %get-tuple-element.16.nv_in.nv, ...), custom_call_target="tpu_custom_call" | custom-call | tf_op jit(solution)/shard_map/tail/pallas_call | solution.py:535
  54.2 0.6 %copy.17 = bf16[8,512]{1,0:T(8,128)(2,1)} copy(bf16[8,512]{1,0:T(8,128)(2,1)S(1)} %tail.1) | data formatting | bytes 16384
Async XLA Ops:
  18.5 4.0 %copy-start = (bf16[512,2048]{1,0:T(8,128)(2,1)S(1)}, bf16[512,2048]{1,0:T(8,128)(2,1)}, u32[]{:S(2)}) copy-start(bf16[512,2048]{1,0:T(8,128)(2,1)} %wo.1) | copy-start | bytes 6291460
  18.5 4.0 %copy-start.1 = (bf16[2048,64]{0,1:T(8,128)(2,1)S(1)}, bf16[2048,64]{0,1:T(8,128)(2,1)}, u32[]{:S(2)}) copy-start(bf16[2048,64]{0,1:T(8,128)(2,1)} %param.20) | copy-start | bytes 786436
  18.5 4.0 %copy-start.2 = (bf16[64,2048]{1,0:T(8,128)(2,1)S(1)}, bf16[64,2048]{1,0:T(8,128)(2,1)}, u32[]{:S(2)}) copy-start(bf16[64,2048]{1,0:T(8,128)(2,1)} %down.1) | copy-start | bytes 786436
  18.5 4.0 %copy-start.3 = (bf16[8,2048]{1,0:T(8,128)(2,1)S(1)}, bf16[8,2048]{1,0:T(8,128)(2,1)}, u32[]{:S(2)}) copy-start(bf16[8,2048]{1,0:T(8,128)(2,1)} %tok.1) | copy-start | bytes 98308
  18.5 4.0 %copy-start.4 = (f32[2048]{0:T(1024)S(1)}, f32[2048]{0:T(1024)}, u32[]{:S(2)}) copy-start(f32[2048]{0:T(1024)} %param.19) | copy-start | bytes 24580

commit v5 on v4

--- a/solution.py
+++ b/solution.py
@@ -13,7 +13,7 @@
 NEG = -1e30
 WIN = 32
 CHUNK = 512
-VMEM_PROJECT, VMEM_ATTEND, VMEM_TAIL = 20 << 20, 16 << 20, 16 << 20
+VMEM_PROJECT, VMEM_FURTHER, VMEM_TAIL = 20 << 20, 12 << 20, 20 << 20
 NT = (((1,), (1,)), ((), ()))
 
 
@@ -90,10 +90,6 @@
     small[0].wait()
     small[1].wait()
     normed = norm(tok[...].astype(jnp.float32), gain[...]).astype(jnp.bfloat16)
-    pl.semaphore_wait(barrier, n + 1)
-    sides = side_copies(up, un, us, ur, me, z, t)
-    for copy in sides:
-        copy.start()
     q = jnp.zeros((tok.shape[0], wq.shape[1]), jnp.float32)
     for i in range(4):
         loads[i].wait()
@@ -103,10 +99,18 @@
     q = (q * HEAD**-0.5).astype(jnp.bfloat16)
     qs[...] = q
     q_all[me] = q
+    pl.semaphore_wait(barrier, n + 1)
     for i, peer in others:
         pltpu.make_async_remote_copy(
             qs, q_all.at[me], ss.at[i], rs.at[me], device_id=(peer, z), device_id_type=MESH
         ).start()
+    half = up.shape[0] // 2
+    sides = side_copies(
+        [up.at[pl.ds(i * half, half)] for i in range(2)], [un.at[i] for i in range(2)],
+        us, ur, me, z, t,
+    )
+    for copy in sides:
+        copy.start()
     loads[4].wait()
     nk[...] = dot(normed, wb[1]).astype(jnp.bfloat16)
     loads[5].wait()
@@ -129,12 +133,16 @@
     tab[2:3] = end
     tab[3:8] = jnp.zeros((5, m), jnp.float32)
 
-    for i, src in others:
+
+    def finish(d):
+        src = lax.rem(me + d, n)
         copy = pltpu.make_async_remote_copy(
-            qs, q_all.at[src], ss.at[i], rs.at[src], device_id=(src, z), device_id_type=MESH
+            qs, q_all.at[src], ss.at[d - 1], rs.at[src], device_id=(src, z), device_id_type=MESH
         )
         copy.wait_recv()
         copy.wait_send()
+
+    each(1, n, finish)
     loads[6].wait()
     loads[7].wait()
     for copy in sides:
@@ -144,43 +152,18 @@
 def side_copies(src, dst, ss, rs, me, z, t):
     return [
         pltpu.make_async_remote_copy(
-            src, dst.at[i], ss.at[i], rs.at[i],
+            src[i], dst[i], ss.at[i], rs.at[i],
             device_id=(me, lax.rem(z + d, t)), device_id_type=MESH,
         )
         for i, d in enumerate((1, t - 1))
     ]
 
 
-def relay_copies(slots, dst, ss, rs, me, z, t):
-    half = dst.shape[0] // 2
-    return [
-        pltpu.make_async_remote_copy(
-            slots.at[i, pl.ds(i * half, half)], dst.at[pl.ds(i * half, half)], ss.at[i], rs.at[i],
-            device_id=(me, lax.rem(z + d, t)), device_id_type=MESH,
-        )
-        for i, d in enumerate((1, t - 1))
-    ]
-
-
-def attend(q_all, tab, nk_in, nv_in, kb, vb, part, nk, nv, sc, acc, put_all):
+def window(slot, base, q_all, tab, kb, vb, sc, acc):
     rows, width = kb.shape
     heads = width // HEAD
-    steps = rows // CHUNK
-    nk[...] = nk_in[...]
-    nv[...] = nv_in[...]
-    base = lax.axis_index("req") * rows
-    base_f = base.astype(jnp.float32)
     rank, first, end = tab[0:1], tab[1:2], tab[2:3]
     m = rank.shape[1]
-    sub = lax.broadcasted_iota(jnp.int32, (m, m), 0)
-    lane = lax.broadcasted_iota(jnp.int32, (m, m), 1)
-    diag = sub == lane
-    upright = lambda row: jnp.sum(jnp.where(diag, row, 0.0), axis=1, keepdims=True)
-    rank_s = upright(rank)
-    here = jnp.logical_and(first < base_f + rows, end > base_f)
-    here_s = upright(jnp.where(here, 1.0, 0.0)) > 0.5
-    low = jnp.min(jnp.where(here, rank, 1e9)).astype(jnp.int32)
-    high = jnp.max(jnp.where(here, rank, -1.0)).astype(jnp.int32)
     every_q = q_all[...].astype(jnp.float32).reshape(m, width).astype(jnp.bfloat16)
     tall = WIN * heads
     block = (
@@ -188,73 +171,122 @@
         == lax.broadcasted_iota(jnp.int32, (tall, width), 1) // HEAD
     )
     spot = lax.broadcasted_iota(jnp.int32, (WIN, HEAD), 1)
-
-    def window(slot, opening):
-        slot_f = slot.astype(jnp.float32)
-        pick = rank == slot_f + lax.broadcasted_iota(jnp.int32, (WIN, m), 0).astype(jnp.float32)
-        pick_f = jnp.where(pick, 1.0, 0.0)
-        q = dot(pick_f.astype(jnp.bfloat16), every_q)
-        first_w = jnp.sum(pick_f * first, axis=1, keepdims=True) - base_f
-        end_w = jnp.sum(pick_f * end, axis=1, keepdims=True) - base_f
-        first_t = jnp.concatenate([first_w] * heads, axis=0)
-        end_t = jnp.concatenate([end_w] * heads, axis=0)
-        q_block = jnp.where(block, jnp.concatenate([q] * heads, axis=0), 0.0).astype(jnp.bfloat16)
-        top = jnp.full((tall, HEAD), NEG, jnp.float32)
-        for i in range(steps):
-            s = lax.dot_general(
-                q_block, kb[i * CHUNK : (i + 1) * CHUNK], NT, preferred_element_type=jnp.float32
-            )
-            at = lax.broadcasted_iota(jnp.int32, (tall, CHUNK), 1).astype(jnp.float32) + float(
-                i * CHUNK
-            )
-            s = jnp.where(jnp.logical_and(at >= first_t, at < end_t), s, NEG)
-            sc[:, i * CHUNK : (i + 1) * CHUNK] = s
-            for j in range(CHUNK // HEAD):
-                top = jnp.maximum(top, s[:, j * HEAD : (j + 1) * HEAD])
-        peak = jnp.max(top, axis=1, keepdims=True)
-        held = jnp.zeros((tall, HEAD), jnp.float32)
-        for i in range(steps):
-            s = sc[:, i * CHUNK : (i + 1) * CHUNK]
-            e = jnp.where(s > 0.1 * NEG, jnp.exp(s - peak), 0.0)
-            for j in range(CHUNK // HEAD):
-                held += e[:, j * HEAD : (j + 1) * HEAD]
-            o = dot(e.astype(jnp.bfloat16), vb[i * CHUNK : (i + 1) * CHUNK])
-            if i == 0:
-                acc[...] = o
-            else:
-                acc[...] += o
-        mass = jnp.sum(held, axis=1, keepdims=True)
-        cut = lambda a, h: a[h * WIN : (h + 1) * WIN]
-        stat = jnp.zeros((WIN, HEAD), jnp.float32)
-        for h in range(heads):
-            stat = jnp.where(spot == h, cut(peak, h), stat)
-            stat = jnp.where(spot == heads + h, cut(mass, h), stat)
-        found = jnp.concatenate(
-            [
-                acc[h * WIN : (h + 1) * WIN, h * HEAD : (h + 1) * HEAD] for h in range(heads)
-            ]
-            + [stat],
-            axis=1,
-        )
-        put = rank_s == slot_f + lax.broadcasted_iota(jnp.int32, (m, WIN), 1).astype(jnp.float32)
-        put = jnp.where(put, 1.0, 0.0).astype(jnp.bfloat16)
-        one = found.astype(jnp.bfloat16)
-        rest = found - one.astype(jnp.float32)
-        two = rest.astype(jnp.bfloat16)
-        three = (rest - two.astype(jnp.float32)).astype(jnp.bfloat16)
-        placed = (dot(put, one) + dot(put, two)) + dot(put, three)
-        if opening:
-            put_all[...] = placed
+    pick = rank == slot + lax.broadcasted_iota(jnp.int32, (WIN, m), 0).astype(jnp.float32)
+    pick = jnp.where(pick, 1.0, 0.0)
+    q = dot(pick.astype(jnp.bfloat16), every_q)
+    first_w = jnp.sum(pick * first, axis=1, keepdims=True) - base
+    end_w = jnp.sum(pick * end, axis=1, keepdims=True) - base
+    first_t = jnp.concatenate([first_w] * heads, axis=0)
+    end_t = jnp.concatenate([end_w] * heads, axis=0)
+    q_block = jnp.where(block, jnp.concatenate([q] * heads, axis=0), 0.0).astype(jnp.bfloat16)
+    top = jnp.full((tall, HEAD), NEG, jnp.float32)
+    for i in range(rows // CHUNK):
+        span = slice(i * CHUNK, (i + 1) * CHUNK)
+        s = lax.dot_general(q_block, kb[span], NT, preferred_element_type=jnp.float32)
+        at = lax.broadcasted_iota(jnp.int32, s.shape, 1).astype(jnp.float32) + float(i * CHUNK)
+        s = jnp.where(jnp.logical_and(at >= first_t, at < end_t), s, NEG)
+        sc[:, span] = s
+        for j in range(CHUNK // HEAD):
+            top = jnp.maximum(top, s[:, j * HEAD : (j + 1) * HEAD])
+    peak = jnp.max(top, axis=1, keepdims=True)
+    held = jnp.zeros((tall, HEAD), jnp.float32)
+    for i in range(rows // CHUNK):
+        span = slice(i * CHUNK, (i + 1) * CHUNK)
+        s = sc[:, span]
+        e = jnp.where(s > 0.1 * NEG, jnp.exp(s - peak), 0.0)
+        for j in range(CHUNK // HEAD):
+            held += e[:, j * HEAD : (j + 1) * HEAD]
+        o = dot(e.astype(jnp.bfloat16), vb[span])
+        if i == 0:
+            acc[...] = o
         else:
-            put_all[...] += placed
-
-    window(low, True)
-    each(1, (high - low) // WIN + 1, lambda w: window(low + w * WIN, False))
-    stat = put_all[:, width:]
+            acc[...] += o
+    mass = jnp.sum(held, axis=1, keepdims=True)
+    cut = lambda a, h: a[h * WIN : (h + 1) * WIN]
+    stat = jnp.zeros((WIN, HEAD), jnp.float32)
+    for h in range(heads):
+        stat = jnp.where(spot == h, cut(peak, h), stat)
+        stat = jnp.where(spot == heads + h, cut(mass, h), stat)
+    found = jnp.concatenate(
+        [acc[h * WIN : (h + 1) * WIN, h * HEAD : (h + 1) * HEAD] for h in range(heads)] + [stat],
+        axis=1,
+    )
+    put = upright(rank) == slot + lax.broadcasted_iota(jnp.int32, (m, WIN), 1).astype(jnp.float32)
+    put = jnp.where(put, 1.0, 0.0).astype(jnp.bfloat16)
+    one = found.astype(jnp.bfloat16)
+    rest = found - one.astype(jnp.float32)
+    two = rest.astype(jnp.bfloat16)
+    three = (rest - two.astype(jnp.float32)).astype(jnp.bfloat16)
+    return (dot(put, one) + dot(put, two)) + dot(put, three)
+
+
+def upright(row):
+    m = row.shape[1]
+    diag = lax.broadcasted_iota(jnp.int32, (m, m), 0) == lax.broadcasted_iota(jnp.int32, (m, m), 1)
+    return jnp.sum(jnp.where(diag, row, 0.0), axis=1, keepdims=True)
+
+
+def present(tab, base, rows):
+    return jnp.logical_and(tab[1:2] < base + rows, tab[2:3] > base)
+
+
+def further(q_all, tab, nk_in, nv_in, kb, vb, more, nk, nv, sc, acc):
+    nk[...] = nk_in[...]
+    nv[...] = nv_in[...]
+    rows = kb.shape[0]
+    base = (lax.axis_index("req") * rows).astype(jnp.float32)
+    rank, here = tab[0:1], present(tab, base, rows)
+    low = jnp.min(jnp.where(here, rank, 1e9)).astype(jnp.int32)
+    high = jnp.max(jnp.where(here, rank, -1.0)).astype(jnp.int32)
+    more[...] = jnp.zeros_like(more)
+
+    def add(w):
+        slot = (low + w * WIN).astype(jnp.float32)
+        more[...] += window(slot, base, q_all, tab, kb, vb, sc, acc)
+
+    each(1, (high - low) // WIN + 1, add)
+
+
+def tail(
+    n, t, more, q_all, tab, kb, vb, nk, nv, un, tok_h, gain_h, wo_h, up, down, hid,
+    sc, acc, part, tok, gain, wo, got, upb, dnb, zs, zr, tp, ns, nr, ts, rr, fs, fr,
+    lsem, a_s, a_r, v_s, v_r, u_s, u_r, d_s, d_r, e_s, e_r, z_s, z_r, n_s, n_r, r_s, r_r, f_s, f_r,
+):
+    me, z = lax.axis_index("req"), lax.axis_index("tp")
+    f32, b16 = jnp.float32, jnp.bfloat16
+    width = q_all.shape[2]
+    heads = width // HEAD
+    own, wide = tok.shape
+    few = own // t
+    half = up.shape[0] // 2
+    loads = [
+        pltpu.make_async_copy(up, upb.at[0], lsem.at[0]),
+        pltpu.make_async_copy(down, dnb.at[0], lsem.at[1]),
+        pltpu.make_async_copy(un.at[0], upb.at[1, pl.ds(0, half)], lsem.at[2]),
+        pltpu.make_async_copy(un.at[1], upb.at[2, pl.ds(half, half)], lsem.at[3]),
+        pltpu.make_async_copy(tok_h, tok, lsem.at[4]),
+        pltpu.make_async_copy(gain_h, gain, lsem.at[5]),
+        pltpu.make_async_copy(wo_h, wo, lsem.at[6]),
+    ]
+    for load in loads:
+        load.start()
+    barrier = pltpu.get_barrier_semaphore()
+
+    others, others_z = line(n, me), ring(t, z)
+    for _, peer in others:
+        pl.semaphore_signal(barrier, inc=1, device_id=(peer, z), device_id_type=MESH)
+    for _, peer in others_z:
+        pl.semaphore_signal(barrier, inc=1, device_id=(me, peer), device_id_type=MESH)
+    base = (me * kb.shape[0]).astype(f32)
+    here = present(tab, base, kb.shape[0])
+    low = jnp.min(jnp.where(here, tab[0:1], 1e9), axis=1, keepdims=True)
+    found = window(low, base, q_all, tab, kb, vb, sc, acc) + more[...]
+    stat = found[:, width:]
     lanes = lax.broadcasted_iota(jnp.int32, stat.shape, 1)
+    here_s = upright(jnp.where(here, 1.0, 0.0)) > 0.5
     stat = jnp.where(jnp.logical_and(lanes < heads, jnp.logical_not(here_s)), NEG, stat)
-    one = stat.astype(jnp.bfloat16).astype(jnp.float32)
-    two = (stat - one).astype(jnp.bfloat16).astype(jnp.float32)
+    one = stat.astype(b16).astype(f32)
+    two = (stat - one).astype(b16).astype(f32)
     three = (stat - one) - two
     kinds = 2 * heads
     stat = jnp.where(
@@ -264,37 +296,8 @@
             lanes < 2 * kinds, pltpu.roll(two, kinds, axis=1), pltpu.roll(three, 2 * kinds, axis=1)
         ),
     )
-    shape = part.shape
-    part[:, :, :width] = put_all[:, :width].reshape(shape[0], shape[1], width).astype(part.dtype)
-    part[:, :, width:] = stat.reshape(shape[0], shape[1], HEAD).astype(part.dtype)
-
-
-def tail(
-    n, t, part, q_all, nk, nv, tok, gain, wo, up, un, down, hid,
-    got, upb, dnb, zs, zr, tp, ns, nr, ts, rr, fs, fr,
-    lsem, a_s, a_r, u_s, u_r, d_s, d_r, e_s, e_r, z_s, z_r, n_s, n_r, r_s, r_r, f_s, f_r,
-):
-    me, z = lax.axis_index("req"), lax.axis_index("tp")
-    f32, b16 = jnp.float32, jnp.bfloat16
-    width = q_all.shape[2]
-    heads = width // HEAD
-    own, wide = tok.shape
-    few = own // t
-    loads = [
-        pltpu.make_async_copy(up, upb.at[0], lsem.at[0]),
-        pltpu.make_async_copy(down, dnb.at[0], lsem.at[1]),
-        pltpu.make_async_copy(part.at[me], got.at[me], lsem.at[2]),
-        pltpu.make_async_copy(un, upb.at[pl.ds(1, 2)], lsem.at[3]),
-    ]
-    for load in loads:
-        load.start()
-    barrier = pltpu.get_barrier_semaphore()
-
-    others, others_z = line(n, me), ring(t, z)
-    for _, peer in others:
-        pl.semaphore_signal(barrier, inc=1, device_id=(peer, z), device_id_type=MESH)
-    for _, peer in others_z:
-        pl.semaphore_signal(barrier, inc=1, device_id=(me, peer), device_id_type=MESH)
+    part[:, :, :width] = found[:, :width].reshape(n, own, width).astype(b16)
+    part[:, :, width:] = stat.reshape(n, own, HEAD).astype(b16)
     pl.semaphore_wait(barrier, n - 1 + t - 1)
 
     def line_copies(src, dst, ss, rs):
@@ -308,10 +311,13 @@
                 one(i, me, peer).start()
 
         def finish():
-            for i, peer in others:
-                copy = one(i, peer, peer)
+            def wait(d):
+                other = lax.rem(me + d, n)
+                copy = one(d - 1, other, other)
                 copy.wait_recv()
                 copy.wait_send()
+
+            each(1, n, wait)
 
         return start, finish
 
@@ -335,11 +341,20 @@
 
     send, take = line_copies(lambda peer: part.at[peer], got, a_s, a_r)
     send()
-    sides = dnb.at[pl.ds(1, 2)]
-    up_relay = relay_copies(un, upb.at[t - 1], u_s, u_r, me, z, t)
-    down_side = side_copies(down, sides, d_s, d_r, me, z, t)
-    down_relay = relay_copies(sides, dnb.at[t - 1], e_s, e_r, me, z, t)
-    for copy in up_relay + down_side:
+    halves = [pl.ds(i * half, half) for i in range(2)]
+    up_side = side_copies(
+        [up.at[halves[1]], up.at[halves[0]]],
+        [upb.at[1, halves[1]], upb.at[2, halves[0]]], v_s, v_r, me, z, t,
+    )
+    down_side = side_copies([down, down], [dnb.at[1], dnb.at[2]], d_s, d_r, me, z, t)
+    up_relay = side_copies(
+        [un.at[0], un.at[1]], [upb.at[t - 1, h] for h in halves], u_s, u_r, me, z, t
+    )
+    down_relay = side_copies(
+        [dnb.at[1, halves[0]], dnb.at[2, halves[1]]], [dnb.at[t - 1, h] for h in halves],
+        e_s, e_r, me, z, t,
+    )
+    for copy in down_side + up_side:
         copy.start()
 
     def pieces(a):
@@ -358,6 +373,8 @@
     for h in range(heads):
         cols = slice(h * HEAD, (h + 1) * HEAD)
         mine = jnp.where(spot == h, jnp.sum(q[:, cols] * kn[:, cols], axis=1, keepdims=True), mine)
+    loads[4].wait()
+    loads[5].wait()
     for k, piece in enumerate(pieces(tok[...].astype(f32))):
         tp[k] = piece
     gains = jnp.concatenate(
@@ -366,9 +383,8 @@
         ],
         axis=0,
     )
-    loads[2].wait()
+    got[me] = part[me]
     take()
-    kinds = 2 * heads
     coded = got[:, :, width:].astype(f32)
     stat = (coded + pltpu.roll(coded, HEAD - kinds, axis=2)) + pltpu.roll(
         coded, HEAD - 2 * kinds, axis=2
@@ -384,6 +400,7 @@
         older = jnp.sum(got[:, :, cols].astype(f32) * scale[:, :, h : h + 1], axis=0)
         attended.append((self_w[:, h : h + 1] * vn[:, cols] + older) / total[:, h : h + 1])
     attended = jnp.concatenate(attended, axis=1).astype(b16)
+    loads[6].wait()
     for k, piece in enumerate(pieces(dot(attended, wo[...]))):
         zs[k] = piece
     send, take = z_copies(lambda peer: zs.at[peer], zr, z_s, z_r)
@@ -393,6 +410,8 @@
     for i in range(1, t):
         mid += zr[lax.rem(z + i, t)]
     mid += tp[z]
+    for copy in up_relay:
+        copy.start()
     for copy in down_side:
         copy.wait()
     for copy in down_relay:
@@ -411,9 +430,9 @@
     nr[me] = normed
     send, take = line_copies(lambda peer: ns, nr, n_s, n_r)
     send()
-    loads[0].wait()
-    loads[3].wait()
-    for copy in up_relay:
+    for i in (0, 2, 3):
+        loads[i].wait()
+    for copy in up_side + up_relay:
         copy.wait()
     take()
     rows, units = n * own, t * up.shape[0]
@@ -471,7 +490,6 @@
     steps = rows // CHUNK
     vmem = pl.BlockSpec(memory_space=pltpu.VMEM)
     hbm = pl.BlockSpec(memory_space=pltpu.HBM)
-    free = pl.BlockSpec(memory_space=pl.ANY)
     dma = pltpu.SemaphoreType.DMA
     shape = jax.ShapeDtypeStruct
     up_rows = up_weight.T
@@ -486,7 +504,7 @@
             shape((8, requests), f32),
             shape((rows, width), b16),
             shape((rows, width), b16),
-            shape((2, units, wide), b16),
+            shape((2, units // 2, wide), b16),
         ),
         in_specs=[hbm] * 10,
         out_specs=(vmem,) * 7,
@@ -515,10 +533,10 @@
             ),
         )
     )
-    part, new_keys, new_values = pl.pallas_call(
-        attend,
+    more, new_keys, new_values = pl.pallas_call(
+        further,
         out_shape=(
-            shape((n, own, width + HEAD), b16),
+            shape((requests, width + HEAD), f32),
             shape((own, width), b16),
             shape((own, width), b16),
         ),
@@ -527,17 +545,22 @@
         scratch_shapes=[
             pltpu.VMEM((WIN * heads, rows), f32),
             pltpu.VMEM((WIN * heads, width), f32),
-            pltpu.VMEM((requests, width + HEAD), f32),
         ],
-        compiler_params=pltpu.CompilerParams(vmem_limit_bytes=VMEM_ATTEND),
-        name="attend",
+        compiler_params=pltpu.CompilerParams(vmem_limit_bytes=VMEM_FURTHER),
+        name="further",
     )(q_all, tab, nk, nv, kb, vb)
     hidden = pl.pallas_call(
         functools.partial(tail, n, t),
         out_shape=shape((own, width), b16),
-        in_specs=[free] + [vmem] * 6 + [free, vmem, free],
+        in_specs=[vmem] * 8 + [hbm] * 5,
         out_specs=vmem,
         scratch_shapes=[
+            pltpu.VMEM((WIN * heads, rows), f32),
+            pltpu.VMEM((WIN * heads, width), f32),
+            pltpu.VMEM((n, own, width + HEAD), b16),
+            pltpu.VMEM((own, wide), b16),
+            pltpu.VMEM((1, wide), f32),
+            pltpu.VMEM((width, wide), b16),
             pltpu.VMEM((n, own, width + HEAD), b16),
             pltpu.VMEM((t, units, wide), b16),
             pltpu.VMEM((t, units, wide), b16),
@@ -550,8 +573,9 @@
             pltpu.VMEM((n, own, width), b16),
             pltpu.VMEM((own, width), b16),
             pltpu.VMEM((t, own, width), b16),
-            dma((4,)),
+            dma((7,)),
             dma((n,)), dma((n,)),
+            dma((2,)), dma((2,)),
             dma((2,)), dma((2,)),
             dma((2,)), dma((2,)),
             dma((2,)), dma((2,)),
@@ -565,8 +589,8 @@
         ),
         name="tail",
     )(
-        part, q_all, nk, nv, tokens,
-        second_gain.reshape(1, wide), out_weight, up_rows, un, down_weight,
+        more, q_all, tab, kb, vb, nk, nv, un,
+        *map(held, (tokens, second_gain.reshape(1, wide), out_weight, up_rows, down_weight)),
     )
     return hidden, new_keys, new_values
 

time: 55.1 us -> 51.2 us (0.929)
  Pallas kernels: 53.5 us -> 49.4 us
    pallas_call x1, Pallas kernels: 3.92 us -> 0.75 us  [body(): pl.pallas_call(further, out_shape=(shape((requests, width + HEAD), f32),...]
    pallas_call x1, Pallas kernels: 17.9 us -> 15.1 us  [body(): pl.pallas_call(functools.partial(project, n, t), out_shape=(shape((n, own...]
    pallas_call x1, Pallas kernels: 31.7 us -> 33.5 us  [body(): pl.pallas_call(functools.partial(tail, n, t), out_shape=shape((own, width...]
where the time goes in v5:
time: 51.2 us; the launch traced here: 50.6 us
  Pallas kernels  49.4 us (96%)
  between operations  0.65 us (1%)
  local copies, waits for them, and re-layouts  0.6 us (1%)
    pallas_call x1, Pallas kernels, body(): pl.pallas_call(functools.partial(tail, n, t), out_shape=shape((own, width...  33.5 us
    pallas_call x1, Pallas kernels, body(): pl.pallas_call(functools.partial(project, n, t), out_shape=(shape((n, own...  15.1 us

profile of v5, /device:TPU:1, one launch (start us, length us, event | category | flops | bytes accessed | tf_op | source)
XLA Modules:
  0.0 50.6 jit_solution(11624363161709161259)
XLA Ops:
  0.6 15.1 %project.1 = (bf16[32,8,512]{2,1,0:T(8,128)(2,1)S(1)}, bf16[8,512]{1,0:T(8,128)(2,1)S(1)}, bf16[8,512]{1,0:T(8,128)(2,1)S(1)}, f32[8,256]{1,0:T(8,128)S(1)}, bf1...) custom-call(bf16[8,2048]{1,0:T(8,128)(2,1)} %tok_h.3, ...), custom_call_target="tpu_custom_call" | custom-call | tf_op jit(solution)/shard_map/project/pallas_call | solution.py:498
  15.8 0.8 %further.1 = (f32[256,640]{1,0:T(8,128)S(1)}, bf16[8,512]{1,0:T(8,128)(2,1)}, bf16[8,512]{1,0:T(8,128)(2,1)}) custom-call(bf16[32,8,512]{2,1,0:T(8,128)(2,1)S(1)} %get-tuple-element.13.q_all, f32[8,256]{1,0:T(8,128)S(1)} %get-tuple-element.14.tab, bf16[8,512]{1,0:T(8,128)(2,1)S(1)} %get-tuple-element.15.nk_in.nk, ...), custom_call_target="tpu_custom_call" | custom-call | tf_op jit(solution)/shard_map/further/pallas_call | solution.py:536
  16.5 33.5 %tail.1 = bf16[8,512]{1,0:T(8,128)(2,1)S(1)} custom-call(f32[256,640]{1,0:T(8,128)S(1)} %get-tuple-element.19.more, bf16[32,8,512]{2,1,0:T(8,128)(2,1)S(1)} %get-tuple-element.13.q_all, f32[8,256]{1,0:T(8,128)S(1)} %get-tuple-element.14.tab, bf16[4096,512]{1,0:T(8,128)(2,1)S(1)} %get-tuple-element.17.kb, bf16[4096,512]{1,0:T(8,128)(2,1)S(1)} %get-tuple-element.18.vb, ...), custom_call_target="tpu_custom_call" | custom-call | tf_op jit(solution)/shard_map/tail/pallas_call | solution.py:552
  50.0 0.6 %copy.17 = bf16[8,512]{1,0:T(8,128)(2,1)} copy(bf16[8,512]{1,0:T(8,128)(2,1)S(1)} %tail.1) | data formatting | bytes 16384

commit v6 on v5

--- a/solution.py
+++ b/solution.py
@@ -102,7 +102,7 @@
     pl.semaphore_wait(barrier, n + 1)
     for i, peer in others:
         pltpu.make_async_remote_copy(
-            qs, q_all.at[me], ss.at[i], rs.at[me], device_id=(peer, z), device_id_type=MESH
+            qs, q_all.at[me], ss.at[0], rs.at[0], device_id=(peer, z), device_id_type=MESH
         ).start()
     half = up.shape[0] // 2
     sides = side_copies(
@@ -133,20 +133,20 @@
     tab[2:3] = end
     tab[3:8] = jnp.zeros((5, m), jnp.float32)
 
-
-    def finish(d):
-        src = lax.rem(me + d, n)
-        copy = pltpu.make_async_remote_copy(
-            qs, q_all.at[src], ss.at[d - 1], rs.at[src], device_id=(src, z), device_id_type=MESH
-        )
-        copy.wait_recv()
-        copy.wait_send()
-
-    each(1, n, finish)
+    queries = together(q_all, n - 1, ss, rs, (others[0][1], z))
+    queries.wait_recv()
+    queries.wait_send()
     loads[6].wait()
     loads[7].wait()
     for copy in sides:
         copy.wait()
+
+
+def together(dst, count, ss, rs, device):
+    slots = dst.at[pl.ds(0, count)]
+    return pltpu.make_async_remote_copy(
+        slots, slots, ss.at[0], rs.at[0], device_id=device, device_id_type=MESH
+    )
 
 
 def side_copies(src, dst, ss, rs, me, z, t):
@@ -300,44 +300,31 @@
     part[:, :, width:] = stat.reshape(n, own, HEAD).astype(b16)
     pl.semaphore_wait(barrier, n - 1 + t - 1)
 
+    sent = []
+
     def line_copies(src, dst, ss, rs):
-        def one(d, s, peer):
-            return pltpu.make_async_remote_copy(
-                src(peer), dst.at[s], ss.at[d], rs.at[s], device_id=(peer, z), device_id_type=MESH
-            )
-
         def start():
-            for i, peer in others:
-                one(i, me, peer).start()
-
-        def finish():
-            def wait(d):
-                other = lax.rem(me + d, n)
-                copy = one(d - 1, other, other)
-                copy.wait_recv()
-                copy.wait_send()
-
-            each(1, n, wait)
-
-        return start, finish
+            for _, peer in others:
+                pltpu.make_async_remote_copy(
+                    src(peer), dst.at[me], ss.at[0], rs.at[0],
+                    device_id=(peer, z), device_id_type=MESH,
+                ).start()
+
+        whole = together(dst, n - 1, ss, rs, (others[0][1], z))
+        sent.append(whole)
+        return start, whole.wait_recv
 
     def z_copies(src, dst, ss, rs):
-        def one(d, s, peer):
-            return pltpu.make_async_remote_copy(
-                src(peer), dst.at[s], ss.at[d], rs.at[s], device_id=(me, peer), device_id_type=MESH
-            )
-
         def start():
-            for d, peer in others_z:
-                one(d, z, peer).start()
-
-        def finish():
-            for d, peer in others_z:
-                copy = one(d, peer, peer)
-                copy.wait_recv()
-                copy.wait_send()
-
-        return start, finish
+            for _, peer in others_z:
+                pltpu.make_async_remote_copy(
+                    src(peer), dst.at[z], ss.at[0], rs.at[0],
+                    device_id=(me, peer), device_id_type=MESH,
+                ).start()
+
+        whole = together(dst, t - 1, ss, rs, (me, others_z[0][1]))
+        sent.append(whole)
+        return start, whole.wait_recv
 
     send, take = line_copies(lambda peer: part.at[peer], got, a_s, a_r)
     send()
@@ -475,6 +462,8 @@
         rows_b = jnp.concatenate([a[b * few : (b + 1) * few] for a in every], axis=0)
         final = jnp.where(z == b, rows_b, final)
     hid[...] = final.astype(b16)
+    for copies in sent:
+        copies.wait_send()
 
 
 def body(
@@ -516,7 +505,7 @@
             pltpu.VMEM((3, wide, width), b16),
             pltpu.VMEM((own, width), b16),
             dma((12,)),
-            dma((n,)), dma((n,)),
+            dma((1,)), dma((1,)),
             dma((2,)), dma((2,)),
         ],
         compiler_params=pltpu.CompilerParams(
@@ -574,15 +563,15 @@
             pltpu.VMEM((own, width), b16),
             pltpu.VMEM((t, own, width), b16),
             dma((7,)),
-            dma((n,)), dma((n,)),
+            dma((1,)), dma((1,)),
             dma((2,)), dma((2,)),
             dma((2,)), dma((2,)),
             dma((2,)), dma((2,)),
             dma((2,)), dma((2,)),
-            dma((t,)), dma((t,)),
-            dma((n,)), dma((n,)),
-            dma((n,)), dma((n,)),
-            dma((t,)), dma((t,)),
+            dma((1,)), dma((1,)),
+            dma((1,)), dma((1,)),
+            dma((1,)), dma((1,)),
+            dma((1,)), dma((1,)),
         ],
         compiler_params=pltpu.CompilerParams(
             collective_id=1, has_side_effects=True, vmem_limit_bytes=VMEM_TAIL

time: 51.2 us -> 48.3 us (0.943)
  Pallas kernels: 49.4 us -> 46.6 us
    pallas_call x1, Pallas kernels: 33.5 us -> 31.3 us  [body(): pl.pallas_call(functools.partial(tail, n, t), out_shape=shape((own, width...]
    pallas_call x1, Pallas kernels: 15.1 us -> 14.6 us  [body(): pl.pallas_call(functools.partial(project, n, t), out_shape=(shape((n, own...]
where the time goes in v6:
time: 48.3 us; the launch traced here: 47.9 us
  Pallas kernels  46.6 us (96%)
  between operations  0.65 us (1%)
  local copies, waits for them, and re-layouts  0.6 us (1%)
    pallas_call x1, Pallas kernels, body(): pl.pallas_call(functools.partial(tail, n, t), out_shape=shape((own, width...  31.3 us
    pallas_call x1, Pallas kernels, body(): pl.pallas_call(functools.partial(project, n, t), out_shape=(shape((n, own...  14.6 us

profile of v6, /device:TPU:1, one launch (start us, length us, event | category | flops | bytes accessed | tf_op | source)
XLA Modules:
  0.0 47.9 jit_solution(11506897213068412152)
XLA Ops:
  0.6 14.6 %project.1 = (bf16[32,8,512]{2,1,0:T(8,128)(2,1)S(1)}, bf16[8,512]{1,0:T(8,128)(2,1)S(1)}, bf16[8,512]{1,0:T(8,128)(2,1)S(1)}, f32[8,256]{1,0:T(8,128)S(1)}, bf1...) custom-call(bf16[8,2048]{1,0:T(8,128)(2,1)} %tok_h.3, ...), custom_call_target="tpu_custom_call" | custom-call | tf_op jit(solution)/shard_map/project/pallas_call | solution.py:487
  15.2 0.8 %further.1 = (f32[256,640]{1,0:T(8,128)S(1)}, bf16[8,512]{1,0:T(8,128)(2,1)}, bf16[8,512]{1,0:T(8,128)(2,1)}) custom-call(bf16[32,8,512]{2,1,0:T(8,128)(2,1)S(1)} %get-tuple-element.13.q_all, f32[8,256]{1,0:T(8,128)S(1)} %get-tuple-element.14.tab, bf16[8,512]{1,0:T(8,128)(2,1)S(1)} %get-tuple-element.15.nk_in.nk, ...), custom_call_target="tpu_custom_call" | custom-call | tf_op jit(solution)/shard_map/further/pallas_call | solution.py:525
  16.0 31.3 %tail.1 = bf16[8,512]{1,0:T(8,128)(2,1)S(1)} custom-call(f32[256,640]{1,0:T(8,128)S(1)} %get-tuple-element.19.more, bf16[32,8,512]{2,1,0:T(8,128)(2,1)S(1)} %get-tuple-element.13.q_all, f32[8,256]{1,0:T(8,128)S(1)} %get-tuple-element.14.tab, bf16[4096,512]{1,0:T(8,128)(2,1)S(1)} %get-tuple-element.17.kb, bf16[4096,512]{1,0:T(8,128)(2,1)S(1)} %get-tuple-element.18.vb, ...), custom_call_target="tpu_custom_call" | custom-call | tf_op jit(solution)/shard_map/tail/pallas_call | solution.py:541
  47.3 0.6 %copy.17 = bf16[8,512]{1,0:T(8,128)(2,1)} copy(bf16[8,512]{1,0:T(8,128)(2,1)S(1)} %tail.1) | data formatting | bytes 16384

commit v7 on v6

--- a/solution.py
+++ b/solution.py
@@ -180,20 +180,22 @@
     end_t = jnp.concatenate([end_w] * heads, axis=0)
     q_block = jnp.where(block, jnp.concatenate([q] * heads, axis=0), 0.0).astype(jnp.bfloat16)
     top = jnp.full((tall, HEAD), NEG, jnp.float32)
+    at = lax.broadcasted_iota(jnp.int32, (tall, CHUNK), 1).astype(jnp.float32)
     for i in range(rows // CHUNK):
         span = slice(i * CHUNK, (i + 1) * CHUNK)
         s = lax.dot_general(q_block, kb[span], NT, preferred_element_type=jnp.float32)
-        at = lax.broadcasted_iota(jnp.int32, s.shape, 1).astype(jnp.float32) + float(i * CHUNK)
-        s = jnp.where(jnp.logical_and(at >= first_t, at < end_t), s, NEG)
+        off = float(i * CHUNK)
+        s = jnp.where(jnp.logical_and(at >= first_t - off, at < end_t - off), s, NEG)
         sc[:, span] = s
         for j in range(CHUNK // HEAD):
             top = jnp.maximum(top, s[:, j * HEAD : (j + 1) * HEAD])
     peak = jnp.max(top, axis=1, keepdims=True)
     held = jnp.zeros((tall, HEAD), jnp.float32)
+    level = jnp.maximum(peak, 0.1 * NEG)
     for i in range(rows // CHUNK):
         span = slice(i * CHUNK, (i + 1) * CHUNK)
         s = sc[:, span]
-        e = jnp.where(s > 0.1 * NEG, jnp.exp(s - peak), 0.0)
+        e = jnp.exp(s - level)
         for j in range(CHUNK // HEAD):
             held += e[:, j * HEAD : (j + 1) * HEAD]
         o = dot(e.astype(jnp.bfloat16), vb[span])
@@ -214,10 +216,11 @@
     put = upright(rank) == slot + lax.broadcasted_iota(jnp.int32, (m, WIN), 1).astype(jnp.float32)
     put = jnp.where(put, 1.0, 0.0).astype(jnp.bfloat16)
     one = found.astype(jnp.bfloat16)
-    rest = found - one.astype(jnp.float32)
+    rest = stat - one[:, width:].astype(jnp.float32)
     two = rest.astype(jnp.bfloat16)
     three = (rest - two.astype(jnp.float32)).astype(jnp.bfloat16)
-    return (dot(put, one) + dot(put, two)) + dot(put, three)
+    exact = (dot(put, one[:, width:]) + dot(put, two)) + dot(put, three)
+    return jnp.concatenate([dot(put, one[:, :width]), exact], axis=1)
 
 
 def upright(row):
@@ -389,13 +392,13 @@
     attended = jnp.concatenate(attended, axis=1).astype(b16)
     loads[6].wait()
     for k, piece in enumerate(pieces(dot(attended, wo[...]))):
-        zs[k] = piece
+        zs[k] = piece.astype(b16)
     send, take = z_copies(lambda peer: zs.at[peer], zr, z_s, z_r)
     send()
-    mid = zs[z]
+    mid = zs[z].astype(f32)
     take()
     for i in range(1, t):
-        mid += zr[lax.rem(z + i, t)]
+        mid += zr[lax.rem(z + i, t)].astype(f32)
     mid += tp[z]
     for copy in up_relay:
         copy.start()
@@ -553,8 +556,8 @@
             pltpu.VMEM((n, own, width + HEAD), b16),
             pltpu.VMEM((t, units, wide), b16),
             pltpu.VMEM((t, units, wide), b16),
-            pltpu.VMEM((t, own, width), f32),
-            pltpu.VMEM((t, own, width), f32),
+            pltpu.VMEM((t, own, width), b16),
+            pltpu.VMEM((t, own, width), b16),
             pltpu.VMEM((t, own, width), f32),
             pltpu.VMEM((own, width), b16),
             pltpu.VMEM((n, own, width), b16),

time: 48.3 us -> 47.8 us (0.990)
  no operation moved by 1% of the time
where the time goes in v7:
time: 47.8 us; the launch traced here: 47.6 us
  Pallas kernels  46.3 us (97%)
  between operations  0.65 us (1%)
  local copies, waits for them, and re-layouts  0.6 us (1%)
    pallas_call x1, Pallas kernels, body(): pl.pallas_call(functools.partial(tail, n, t), out_shape=shape((own, width...  31 us
    pallas_call x1, Pallas kernels, body(): pl.pallas_call(functools.partial(project, n, t), out_shape=(shape((n, own...  14.6 us

profile of v7, /device:TPU:1, one launch (start us, length us, event | category | flops | bytes accessed | tf_op | source)
XLA Modules:
  0.0 47.6 jit_solution(2981452252770752744)
XLA Ops:
  0.6 14.6 %project.1 = (bf16[32,8,512]{2,1,0:T(8,128)(2,1)S(1)}, bf16[8,512]{1,0:T(8,128)(2,1)S(1)}, bf16[8,512]{1,0:T(8,128)(2,1)S(1)}, f32[8,256]{1,0:T(8,128)S(1)}, bf1...) custom-call(bf16[8,2048]{1,0:T(8,128)(2,1)} %tok_h.3, ...), custom_call_target="tpu_custom_call" | custom-call | tf_op jit(solution)/shard_map/project/pallas_call | solution.py:490
  15.2 0.8 %further.1 = (f32[256,640]{1,0:T(8,128)S(1)}, bf16[8,512]{1,0:T(8,128)(2,1)}, bf16[8,512]{1,0:T(8,128)(2,1)}) custom-call(bf16[32,8,512]{2,1,0:T(8,128)(2,1)S(1)} %get-tuple-element.13.q_all, f32[8,256]{1,0:T(8,128)S(1)} %get-tuple-element.14.tab, bf16[8,512]{1,0:T(8,128)(2,1)S(1)} %get-tuple-element.15.nk_in.nk, ...), custom_call_target="tpu_custom_call" | custom-call | tf_op jit(solution)/shard_map/further/pallas_call | solution.py:528
  16.0 31.0 %tail.1 = bf16[8,512]{1,0:T(8,128)(2,1)S(1)} custom-call(f32[256,640]{1,0:T(8,128)S(1)} %get-tuple-element.19.more, bf16[32,8,512]{2,1,0:T(8,128)(2,1)S(1)} %get-tuple-element.13.q_all, f32[8,256]{1,0:T(8,128)S(1)} %get-tuple-element.14.tab, bf16[4096,512]{1,0:T(8,128)(2,1)S(1)} %get-tuple-element.17.kb, bf16[4096,512]{1,0:T(8,128)(2,1)S(1)} %get-tuple-element.18.vb, ...), custom_call_target="tpu_custom_call" | custom-call | tf_op jit(solution)/shard_map/tail/pallas_call | solution.py:544
  47.0 0.6 %copy.17 = bf16[8,512]{1,0:T(8,128)(2,1)} copy(bf16[8,512]{1,0:T(8,128)(2,1)S(1)} %tail.1) | data formatting | bytes 16384
